TPU v7x, 128 devices: a whole 4x4x4 slice. The times are simulated.
128 devices in a mesh: rec: 4 (over z), tm: 32 (over x, y, core).
Axes of the slice: x: 4, y: 4, z: 4, core: 2. Of those that a mesh axis runs over, the one named last changes fastest.
Arguments:
- mel_frames: bfloat16 [4, 65536, 80], P('rec', 'tm'), may hold values from -6 to 6
- lengths: int32 [4, 4], P('rec'), may hold values from 1 to 32768, 65536 in all within a row
- w_first: float32 [3, 3, 256], replicated, may hold values from -2 to 2
- w_second: bfloat16 [2304, 256], P(('rec', 'tm')), may hold values from -0.125 to 0.125
- w_proj: bfloat16 [5120, 1024], P(('rec', 'tm')), may hold values from -0.078125 to 0.078125
- gain_attn: float32 [1024], replicated, may hold values from 0.5 to 1.5
- w_qkv: bfloat16 [1024, 3072], P(('rec', 'tm')), may hold values from -2 to 2
- w_out: bfloat16 [1024, 1024], P(('rec', 'tm')), may hold values from -0.1875 to 0.1875
- gain_conv: float32 [1024], replicated, may hold values from 0.5 to 1.5
- w_point_in: bfloat16 [1024, 2048], P(('rec', 'tm')), may hold values from -0.1875 to 0.1875
- w_depth: float32 [9, 1024], replicated, may hold values from -6 to 6
- w_point_out: bfloat16 [1024, 1024], P(('rec', 'tm')), may hold values from -0.375 to 0.375
- gain_out: float32 [1024], replicated, may hold values from 0.5 to 1.5
Outputs:
- encoded: bfloat16 [4, 16384, 1024], P('rec', 'tm')
Inputs may be any that keep to these rules, and one draw needn't show every extreme that they name: Each group's 4 lengths sum to 65536, and the largest of them is 32768.
All inputs are finite; a program needn't handle non-finite values.
Results may differ from a plain program's by a relative error of at most 0.024.
The roundings to bfloat16 on the way count: a program that leaves them out, or rounds other values in their place, can miss the bound.
Values may be sent and summed in bfloat16 or wider, within the bound.
A program may use at most 128 MiB of HBM per device.

v0:
```python
import jax
import jax.numpy as jnp
from jax import lax
from jax.sharding import PartitionSpec as P

WIDTH = 1024
HEADS = 8
KERNEL = 9
WINDOW = 128
CONV_BLOCK = 64
HEAD_DIM = 128


NORM_EPSILON = 1e-05


def passed_along(block, axis, distance):
    devices = range(lax.axis_size(axis))
    route = [(i - distance, i) for i in devices if i - distance in devices]
    return lax.ppermute(block, axis, route)


def with_halo(block, sides, width):
    for axis, dim in sides:
        count = lax.axis_size(axis)
        forward = [(i, i + 1) for i in range(count - 1)]
        backward = [(target, source) for source, target in forward]
        low = lax.ppermute(
            lax.slice_in_dim(block, block.shape[dim] - width, None, axis=dim), axis, forward
        )
        high = lax.ppermute(lax.slice_in_dim(block, 0, width, axis=dim), axis, backward)
        block = jnp.concatenate([low, block, high], axis=dim)
    return block


def layer_norm(values, gain):
    row_mean = jnp.mean(values, axis=-1, keepdims=True)
    centred = values - row_mean
    variance = jnp.mean(centred * centred, axis=-1, keepdims=True)
    return centred * lax.rsqrt(variance + NORM_EPSILON) * gain


def segment_ids(positions, bounds, limit):
    counted = jnp.sum((positions[:, None] >= bounds[None, :-1]).astype(jnp.int32), axis=1)
    inside = (positions >= 0) & (positions < limit)
    return jnp.where(inside, counted, -1)


def conv_first(window, seg_rows, w_first):
    frame_count = (window.shape[0] - 1) // 2
    bins = window.shape[1]
    padded = jnp.pad(window.astype(jnp.float32), ((0, 0), (1, 1)))
    centre = seg_rows[1 : 2 * frame_count : 2]
    total = jnp.zeros((frame_count, bins // 2, w_first.shape[-1]), jnp.float32)
    for step_t in range(3):
        taken = padded[step_t : step_t + 2 * frame_count - 1 : 2]
        same_seg = (seg_rows[step_t : step_t + 2 * frame_count - 1 : 2] == centre).astype(
            jnp.float32
        )
        taken = taken * same_seg[:, None]
        for step_f in range(3):
            columns = taken[:, step_f : step_f + bins - 1 : 2]
            total = total + columns[:, :, None] * w_first[step_t, step_f][None, None, :]
    return jnp.maximum(total, 0.0).astype(jnp.bfloat16)


def conv_second(first, seg_first, w_second):
    frame_count = (first.shape[0] - 1) // 2
    channels = first.shape[2]
    quarter = first.shape[1] // 2
    padded = jnp.pad(first, ((0, 0), (1, 1), (0, 0)))
    centre = seg_first[1 : 2 * frame_count : 2]
    total = jnp.zeros((frame_count * quarter, w_second.shape[1]), jnp.float32)
    for step_t in range(3):
        taken = padded[step_t : step_t + 2 * frame_count - 1 : 2]
        same_seg = (seg_first[step_t : step_t + 2 * frame_count - 1 : 2] == centre).astype(
            jnp.bfloat16
        )
        taken = taken * same_seg[:, None, None]
        for step_f in range(3):
            columns = taken[:, step_f : step_f + 2 * quarter - 1 : 2].reshape(
                frame_count * quarter, channels
            )
            offset = (step_t * 3 + step_f) * channels
            total = total + jnp.dot(
                columns, w_second[offset : offset + channels], preferred_element_type=jnp.float32
            )
    return jnp.maximum(total, 0.0).astype(jnp.bfloat16).reshape(frame_count, quarter * channels)


def attend_block(q_block, kv_block, q_seg, k_seg):
    row_count = q_block.shape[0]
    span = kv_block.shape[0]
    reach = (span - row_count) // 2
    offsets = (
        jnp.arange(span, dtype=jnp.int32)[None, :]
        - jnp.arange(row_count, dtype=jnp.int32)[:, None]
        - reach
    )
    allowed = (jnp.abs(offsets) <= reach) & (k_seg[None, :] == q_seg[:, None])

    def one_head(head):
        start = head * HEAD_DIM
        q_head = lax.dynamic_slice_in_dim(q_block, start, HEAD_DIM, 1)
        k_head = lax.dynamic_slice_in_dim(kv_block, start, HEAD_DIM, 1)
        v_head = lax.dynamic_slice_in_dim(kv_block, WIDTH + start, HEAD_DIM, 1)
        scores = lax.dot_general(
            q_head, k_head, (((1,), (1,)), ((), ())), preferred_element_type=jnp.float32
        ) * HEAD_DIM ** (-0.5)
        scores = jnp.where(allowed, scores, -1e30)
        row_max = jnp.max(scores, axis=-1, keepdims=True)
        exped = jnp.where(allowed, jnp.exp(scores - row_max), 0.0)
        probabilities = (exped / jnp.sum(exped, axis=-1, keepdims=True)).astype(jnp.bfloat16)
        return jnp.dot(probabilities, v_head, preferred_element_type=jnp.float32).astype(
            jnp.bfloat16
        )

    per_head = lax.map(one_head, jnp.arange(HEADS, dtype=jnp.int32))
    return jnp.transpose(per_head, (1, 0, 2)).reshape(row_count, WIDTH)


def depthwise(gated_ext, seg_ext, seg_mid, w_depth):
    length = seg_mid.shape[0]
    total = jnp.zeros((length, gated_ext.shape[1]), jnp.float32)
    for tap_index in range(w_depth.shape[0]):
        same_seg = (seg_ext[tap_index : tap_index + length] == seg_mid).astype(jnp.float32)
        total = (
            total
            + gated_ext[tap_index : tap_index + length].astype(jnp.float32)
            * w_depth[tap_index][None, :]
            * same_seg[:, None]
        )
    return jax.nn.silu(total).astype(jnp.bfloat16)


def add_product(inputs, piece):
    return jnp.dot(inputs, piece, preferred_element_type=jnp.float32)


def on_device(
    mel_frames,
    lengths,
    w_first,
    w_second,
    w_proj,
    gain_attn,
    w_qkv,
    w_out,
    gain_conv,
    w_point_in,
    w_depth,
    w_point_out,
    gain_out,
):
    frames_dev = mel_frames.shape[1]
    tokens_dev = frames_dev // 4
    shards = lax.axis_size("tm")
    index = lax.axis_index("tm")
    frames_all = frames_dev * shards
    bounds = jnp.cumsum(lengths[0])
    local_mel = mel_frames[0]
    first_base = index * frames_dev
    second_full = lax.all_gather(w_second, ("rec", "tm"), axis=0, tiled=True)
    block_count = tokens_dev // CONV_BLOCK
    mel_edge = passed_along(local_mel[frames_dev - 3 :], "tm", 1)
    extended = jnp.concatenate([mel_edge, local_mel], axis=0)

    def sub_block(block):
        start = block * CONV_BLOCK
        window = lax.dynamic_slice_in_dim(extended, 4 * start, 4 * CONV_BLOCK + 3, 0)
        positions = first_base + 4 * start - 3 + jnp.arange(4 * CONV_BLOCK + 3, dtype=jnp.int32)
        seg_rows = segment_ids(positions, bounds, frames_all)
        first = conv_first(window, seg_rows, w_first)
        return conv_second(first, seg_rows[1::2], second_full)

    sub = lax.map(sub_block, jnp.arange(block_count, dtype=jnp.int32))
    sub = sub.reshape(tokens_dev, sub.shape[-1])
    hidden = add_product(sub, lax.all_gather(w_proj, ("rec", "tm"), axis=0, tiled=True))
    token_pos = index * tokens_dev + jnp.arange(tokens_dev, dtype=jnp.int32)
    token_seg = segment_ids(4 * token_pos, bounds, frames_all)
    key_pos = index * tokens_dev - WINDOW + jnp.arange(tokens_dev + 2 * WINDOW, dtype=jnp.int32)
    key_seg = segment_ids(4 * key_pos, bounds, frames_all)
    normed = layer_norm(hidden, gain_attn).astype(jnp.bfloat16)
    mixed = add_product(normed, lax.all_gather(w_qkv, ("rec", "tm"), axis=0, tiled=True)).astype(
        jnp.bfloat16
    )
    query = mixed[:, :WIDTH]
    keyval = with_halo(mixed[:, WIDTH:], (("tm", 0),), WINDOW)
    block_rows = min(512, tokens_dev)
    block = 0
    start = block * block_rows
    pieces = attend_block(query, keyval, token_seg, key_seg)
    attn_out = add_product(pieces, lax.all_gather(w_out, ("rec", "tm"), axis=0, tiled=True))
    attended = hidden + attn_out
    normed_conv = layer_norm(attended, gain_conv).astype(jnp.bfloat16)
    upward = add_product(normed_conv, lax.all_gather(w_point_in, ("rec", "tm"), axis=0, tiled=True))
    gated = (upward[:, :WIDTH] * jax.nn.sigmoid(upward[:, WIDTH:])).astype(jnp.bfloat16)
    reach = KERNEL // 2
    gated_ext = with_halo(gated, (("tm", 0),), KERNEL // 2)
    depth_pos = index * tokens_dev - reach + jnp.arange(tokens_dev + 2 * reach, dtype=jnp.int32)
    seg_ext = segment_ids(4 * depth_pos, bounds, frames_all)
    acted = depthwise(gated_ext, seg_ext, token_seg, w_depth)
    conv_out = add_product(acted, lax.all_gather(w_point_out, ("rec", "tm"), axis=0, tiled=True))
    combined = attended + conv_out
    return layer_norm(combined, gain_out).astype(jnp.bfloat16)[None]


def solution(mesh):
    placed = (
        P("rec", "tm", None),
        P("rec", None),
        P(),
        P(("rec", "tm"), None),
        P(("rec", "tm"), None),
        P(),
        P(("rec", "tm"), None),
        P(("rec", "tm"), None),
        P(),
        P(("rec", "tm"), None),
        P(),
        P(("rec", "tm"), None),
        P(),
    )
    return jax.shard_map(
        on_device, mesh=mesh, in_specs=placed, out_specs=P("rec", "tm", None), check_vma=False
    )
```

profile of v0, /device:TPU:0, one launch (start us, length us, event | category | flops | bytes accessed | tf_op | source)
XLA Modules:
  0.0 874.0 jit_solution(9001724628954924536)
XLA Ops:
  16.9 59.9 %all-gather.18.cloned.1.call-done = bf16[128,18,256]{2,1,0:T(8,128)(2,1)} async-done(((bf16[1,18,256]{2,1,0:T(8,128)(2,1)}), bf16[128,18,256]{2,1,0:T(8,128)(2,1)}) %all-gather.18.cloned.1.call-update) | async-done | bytes 1179664 | tf_op jit(solution)/shard_map/all_gather | solution.py:163
  80.6 684.0 %while.25 = (s32[]{:T(128)}, bf16[8,64,5120]{2,1,0:T(8,128)(2,1)}, s32[8]{0:T(128)}, bf16[2051,80]{1,0:T(8,128)(2,1)}, s32[]{:T(128)}, /*index=5*/s32[4]{0:T(128...) while((s32[]{:T(128)}, bf16[8,64,5120]{2,1,0:T(8,128)(2,1)}, ...), condition=%wide.region_3.4_spmd, body=%wide.region_1.3_spmd.sunk | while | flops 1543876352 | bytes 92566552 | solution.py:176
  92.3 7.7 maximum_convert_fusion.2
  103.6 6.9 slice.735
  116.4 4.9 slice.737
  125.0 4.8 slice.738
  136.8 4.9 slice.740
  145.5 4.8 slice.741
  157.2 4.9 slice.743
  177.9 7.7 maximum_convert_fusion.2
  189.3 6.9 slice.735
  202.0 4.9 slice.737
  210.6 4.8 slice.738
  222.3 4.9 slice.740
  231.0 4.8 slice.741
  242.6 4.9 slice.743
  263.3 7.7 maximum_convert_fusion.2
  274.8 6.9 slice.735
  287.5 4.9 slice.737
  296.1 4.8 slice.738
  307.8 4.9 slice.740
  316.4 4.8 slice.741
  328.1 4.9 slice.743
  348.9 7.7 maximum_convert_fusion.2
  360.3 6.9 slice.735
  373.1 4.9 slice.737
  381.6 4.8 slice.738
  393.4 4.9 slice.740
  402.0 4.8 slice.741
  413.7 4.9 slice.743
  434.4 7.7 maximum_convert_fusion.2
  445.8 6.9 slice.735
  458.6 4.9 slice.737
  467.1 4.8 slice.738
  478.9 4.9 slice.740
  487.5 4.8 slice.741
  499.2 4.9 slice.743
  519.9 7.7 maximum_convert_fusion.2
  531.3 6.9 slice.735
  544.0 4.9 slice.737
  552.6 4.8 slice.738
  564.3 4.9 slice.740
  573.0 4.8 slice.741
  584.7 4.9 slice.743
  605.4 7.7 maximum_convert_fusion.2
  616.7 6.9 slice.735
  629.5 4.9 slice.737
  638.1 4.8 slice.738
  649.8 4.9 slice.740
  658.4 4.8 slice.741
  670.1 4.9 slice.743
  690.8 7.7 maximum_convert_fusion.2
  702.2 6.9 slice.735
  715.0 4.9 slice.737
  723.5 4.8 slice.738
  735.3 4.9 slice.740
  743.9 4.8 slice.741
  755.6 4.9 slice.743
  764.6 10.0 %fusion.62 = (f32[512]{0:T(512)S(1)}, f32[512,1024]{1,0:T(8,128)S(1)}) fusion(bf16[512,5120]{1,0:T(8,128)(2,1)} %bitcast.117, bf16[5120,1024]{1,0:T(8,128)(2,1)} %all-gather.8.cloned.1.call-done), kind=kOutput, calls=%fused_computation.140 | convolution fusion | flops 5369232896 | bytes 17827840 | tf_op jit(solution)/shard_map/dot_general | solution.py:137
  775.3 6.6 convolution_convert_fusion.1
  790.0 47.7 %while.26 = (s32[]{:T(128)}, bf16[8,512,128]{1,2,0:T(8,128)(2,1)}, s32[8]{0:T(128)S(1)}, bf16[512,1024]{1,0:T(8,128)(2,1)S(1)}, bf16[768,2048]{1,0:T(8,128)(2,1)...) while((s32[]{:T(128)}, bf16[8,512,128]{1,2,0:T(8,128)(2,1)}, ...), condition=%wide.region_11.12_spmd.clone, body=%wide.region_8.11_spmd.clone.sunk | while | flops 212401152 | bytes 5925630 | solution.py:118
  842.2 4.6 fusion.38
  847.4 8.7 collective-permute-start.3
  859.2 6.0 fusion.64
  (639 shorter events, 441.6 us)
Async XLA Ops:
  6.5 70.3 %all-gather.18.cloned.1.call-start = ((), (), s32[]{:S(2)}) async-start(), calls=%async_computation.5 | async-start | bytes 1585152 | tf_op jit(solution)/shard_map/all_gather | solution.py:163
  7.3 757.3 %all-gather.8.cloned.1.call-start = ((), (), s32[]{:S(2)}) async-start(), calls=%async_computation | async-start | bytes 10567680 | tf_op jit(solution)/shard_map/all_gather | solution.py:178
  8.0 767.0 %all-gather.10.cloned.1.call-start = ((), (), s32[]{:S(2)}) async-start(), calls=%async_computation.1 | async-start | bytes 6340608 | tf_op jit(solution)/shard_map/all_gather | solution.py:184
  8.7 828.9 %all-gather.12.cloned.1.call-start = ((), (), s32[]{:S(2)}) async-start(), calls=%async_computation.2 | async-start | bytes 2113536 | tf_op jit(solution)/shard_map/all_gather | solution.py:193
  9.3 832.6 %all-gather.14.cloned.1.call-start = ((), (), s32[]{:S(2)}) async-start(), calls=%async_computation.3 | async-start | bytes 4227072 | tf_op jit(solution)/shard_map/all_gather | solution.py:196
  9.9 847.8 %all-gather.16.cloned.1.call-start = ((), (), s32[]{:S(2)}) async-start(), calls=%async_computation.4 | async-start | bytes 2113536 | tf_op jit(solution)/shard_map/all_gather | solution.py:203
  11.2 69.4 %copy-start.7 = (f32[3,3,256]{2,1,0:T(4,128)S(1)}, f32[3,3,256]{2,1,0:T(4,128)}, u32[]{:S(2)}) copy-start(f32[3,3,256]{2,1,0:T(4,128)} %param.19) | copy-start | bytes 27652
  11.2 4.7 collective-permute-start
  14.5 66.1 %copy-start.11 = (s32[3]{0:T(128)}, s32[3]{0:T(128)S(1)}, u32[]{:S(2)}) copy-start(s32[3]{0:T(128)S(1)} %slice_bitcast_fusion.1) | copy-start | bytes 40
  110.5 2.5 copy-start.2
  121.3 3.7 copy-start.1
  125.0 6.0 copy-start.4
  141.7 3.8 copy-start
  145.5 6.0 copy-start.3
  196.1 2.5 copy-start.2
  206.9 3.7 copy-start.1
  210.6 6.0 copy-start.4
  227.3 3.7 copy-start
  230.9 6.0 copy-start.3
  281.6 2.5 copy-start.2
  292.4 3.7 copy-start.1
  296.1 6.0 copy-start.4
  312.7 3.7 copy-start
  316.4 6.0 copy-start.3
  367.2 2.5 copy-start.2
  378.0 3.7 copy-start.1
  381.6 6.0 copy-start.4
  398.3 3.7 copy-start
  402.0 6.0 copy-start.3
  452.7 2.5 copy-start.2
  463.5 3.7 copy-start.1
  467.1 6.0 copy-start.4
  483.8 3.7 copy-start
  487.5 6.0 copy-start.3
  538.1 2.5 copy-start.2
  548.9 3.7 copy-start.1
  552.6 6.0 copy-start.4
  569.3 3.7 copy-start
  573.0 6.0 copy-start.3
  623.6 2.5 copy-start.2
  634.4 3.7 copy-start.1
  638.1 6.0 copy-start.4
  654.7 3.7 copy-start
  658.4 6.0 copy-start.3
  709.1 2.5 copy-start.2
  719.8 3.7 copy-start.1
  723.5 6.0 copy-start.4
  740.2 3.7 copy-start
  743.9 6.0 copy-start.3
  774.6 7.3 copy-start.6
  774.6 0.7 copy-start.14
  781.9 4.1 copy-start.5
  781.9 3.8 copy-start.10
  781.9 3.8 copy-start.12
  781.9 3.9 copy-start.8
  781.9 3.9 copy-start.9
  782.0 4.0 collective-permute-start.1
  784.4 3.8 collective-permute-start.2
  786.0 3.9 slice-start
  841.6 0.7 copy-start.15
  847.4 10.3 %collective-permute-start.3 = (bf16[4,1024]{1,0:T(4,128)(2,1)S(1)}, bf16[4,1024]{1,0:T(4,128)(2,1)S(1)}, u32[]{:S(2)}, u32[]{:S(2)}) collective-permute-start(bf16[4,1024]{1,0:T(4,128)(2,1)S(1)} %get-tuple-element.260), channel_id=1, source_target_pairs={{0,1},{1,2},{2,3},{3,4},{4,5},{5,6},{6,7},{7,8},{8,9},{9,10},{10,1... | collective-permute-start | bytes 24584 | tf_op jit(solution)/shard_map/ppermute | solution.py:28
  856.1 3.1 collective-permute-start.4
  865.2 0.7 copy-start.13
Sparse Core Ops, SparseCore 0:
  10.2 66.6 all-gather.17
  80.0 69.0 all-gather.7
  152.2 66.3 all-gather.9
  221.6 62.9 all-gather.11
  287.5 64.2 all-gather.13
  354.9 62.7 all-gather.15
where the time goes:
time: 886 us; the launch traced here: 874 us
  local copies, waits for them, and re-layouts  458 us (52%)
  matrix products  202 us (23%)
  other arithmetic  106 us (12%)
  waiting for transfers between devices  66.7 us (8%)
  starting transfers between devices  15.3 us (2%)
  between operations  13.8 us (2%)
  loops' own time  12.5 us (1%)
    slice x72, local copies, waits for them, and re-layouts, conv_second(): taken[:, step_f:step_f + 2 * quarter - 1:2]  284 us
    dot_general x72, matrix products, conv_second(): jnp.dot(columns, w_second[offset:offset + channels], preferred_element_ty...  145 us
    convert_element_type x8, other arithmetic, conv_first(): return jnp.maximum(total, 0.0).astype(jnp.bfloat16)  61.5 us
    all_gather x1, waiting for transfers between devices, on_device(): second_full = lax.all_gather(w_second, ('rec', 'tm'), axis=0, tiled=True)  59.9 us
    slice x72, local copies, waits for them, and re-layouts, conv_first(): columns = taken[:, step_f:step_f + bins - 1:2]  57.2 us
    reshape x72, local copies, waits for them, and re-layouts, conv_second(): taken[:, step_f:step_f + 2 * quarter - 1:2]  56 us
    dot_general x5, matrix products, add_product(): return jnp.dot(inputs, piece, preferred_element_type=jnp.float32)  31 us
    mul x8, other arithmetic, conv_second(): taken = taken * same_seg[:, None, None]  23.8 us
  transfers between devices with their start and end apart: 11, of which 3 were waited for; matrix products, arithmetic and copies ran while one was open for 87% of the time, Pallas kernels for 0%

commit v1 on v0

v1 whole, which is shorter than its diff:
```python
import jax, jax.numpy as jnp
from jax import lax
from jax.experimental import pallas as pl
from jax.experimental.pallas import tpu as pltpu
from jax.sharding import PartitionSpec as P

MESH = pl.DeviceIdType.MESH
AXES = {"z": 0, "x": 1, "y": 2}
ORDERS = (("x", "y", "z"), ("y", "z", "x"), ("z", "x", "y"))
CHUNKS = (
    (0, 0, 256, 0), (1, 0, 256, 0), (1, 256, 384, 1), (1, 640, 384, 2),
    (2, 0, 1024, 0), (2, 1024, 1024, 1), (2, 2048, 1024, 2),
    (3, 0, 1024, 0), (4, 0, 384, 0), (5, 0, 1024, 1), (4, 384, 384, 1), (4, 768, 1280, 2),
)

def gather_kernel(*refs):
    n = 6
    ins, outs = refs[:n], refs[n:2 * n]
    send_sems, recv_sems, sib_send, sib_recv, local_sems = refs[2 * n:]
    z = lax.axis_index("rec")
    tm = lax.axis_index("tm")
    x, y, c = tm // 8, (tm // 2) % 4, tm % 2
    here = {"z": z, "x": x, "y": y}

    def device(pos, core):
        return {"rec": pos["z"], "tm": pos["x"] * 8 + pos["y"] * 2 + core}

    def moved(axis, step):
        pos = dict(here)
        pos[axis] = (here[axis] + step + 4) % 4
        return pos

    def place(order, stage, pos, core, half=None):
        free = ORDERS[order][: stage - 1]
        index = []
        for axis in ("z", "x", "y"):
            if axis not in free:
                index.append(pos[axis])
            elif half is not None and axis == free[0]:
                index.append(pl.ds(2 * half, 2))
            else:
                index.append(slice(None))
        return tuple(index) + (core,)

    barrier = pltpu.get_barrier_semaphore()
    for axis in ("x", "y", "z"):
        for step in (1, 2, 3):
            pl.semaphore_signal(barrier, inc=1, device_id=device(moved(axis, step), c), device_id_type=MESH)
    pl.semaphore_signal(barrier, inc=1, device_id=device(here, 1 - c), device_id_type=MESH)

    local = []
    for a in range(n):
        copy = pltpu.make_async_copy(ins[a], outs[a].at[z, x, y, c], local_sems.at[a])
        copy.start()
        local.append(copy)
    pl.semaphore_wait(barrier, 10)

    everything = []

    def remote(chunk, src, dst, slot, target):
        copy = pltpu.make_async_remote_copy(
            src_ref=src, dst_ref=dst, send_sem=send_sems.at[chunk, slot],
            recv_sem=recv_sems.at[chunk, slot], device_id=target, device_id_type=MESH)
        copy.start()
        everything.append(copy)
        return copy

    def view(chunk, index):
        a, col, cols, order = CHUNKS[chunk]
        return outs[a].at[index + (slice(None), pl.ds(col, cols))]

    def sibling(chunk, slot, stage, pos, half=None):
        order = CHUNKS[chunk][3]
        ref = view(chunk, place(order, stage, pos, c, half))
        copy = pltpu.make_async_remote_copy(
            src_ref=ref, dst_ref=ref, send_sem=sib_send.at[chunk, slot],
            recv_sem=sib_recv.at[chunk, slot], device_id=device(here, 1 - c), device_id_type=MESH)
        copy.start()
        everything.append(copy)
        return copy

    m = len(CHUNKS)
    first, second, second_b, third, third_b, sib = {}, {}, {}, {}, {}, {}
    for k, (a, col, cols, order) in enumerate(CHUNKS):
        axis = ORDERS[order][0]
        src = ins[a].at[:, pl.ds(col, cols)]
        dst = view(k, place(order, 1, here, c))
        first[k] = [remote(k, src, dst, i, device(moved(axis, step), c)) for i, step in enumerate((1, 3, 2))]
    for copy in local:
        copy.wait()
    for stage, base, store, store_b in ((2, 3, second, second_b), (3, 7, third, third_b)):
        for k, (a, col, cols, order) in enumerate(CHUNKS):
            axis = ORDERS[order][stage - 1]
            for copy in (first[k] if stage == 2 else second_b[k]):
                copy.wait_recv()
            ref = view(k, place(order, stage, here, c))
            store[k] = [remote(k, ref, ref, base + i, device(moved(axis, step), c)) for i, step in enumerate((1, 3))]
            if stage == 3:
                sib[k] = [sibling(k, 0, 3, here)]
        for k, (a, col, cols, order) in enumerate(CHUNKS):
            axis = ORDERS[order][stage - 1]
            for copy in store[k]:
                copy.wait_recv()
            store_b[k] = []
            for i, (came, goes) in enumerate(((3, 1), (1, 3))):
                ref = view(k, place(order, stage, moved(axis, came), c, i))
                store_b[k].append(remote(k, ref, ref, base + 2 + i, device(moved(axis, goes), c)))
            if stage == 3:
                sib[k].append(sibling(k, 1, 3, moved(axis, 3)))
                sib[k].append(sibling(k, 2, 3, moved(axis, 1)))
    for k, (a, col, cols, order) in enumerate(CHUNKS):
        axis = ORDERS[order][2]
        for copy in third_b[k]:
            copy.wait_recv()
        sib[k].append(sibling(k, 3, 3, moved(axis, 2)))
    for k in range(m):
        for copy in sib[k]:
            copy.wait_recv()
    for copy in everything:
        copy.wait_send()

def gather_all(shards):
    m = len(CHUNKS)
    return pl.pallas_call(
        gather_kernel,
        out_shape=[jax.ShapeDtypeStruct((4, 4, 4, 2) + s.shape, s.dtype) for s in shards],
        in_specs=[pl.BlockSpec(memory_space=pl.ANY)] * 6,
        out_specs=[pl.BlockSpec(memory_space=pl.ANY)] * 6,
        scratch_shapes=[
            pltpu.SemaphoreType.DMA((m, 11)), pltpu.SemaphoreType.DMA((m, 11)),
            pltpu.SemaphoreType.DMA((m, 4)), pltpu.SemaphoreType.DMA((m, 4)),
            pltpu.SemaphoreType.DMA((6,)),
        ],
        compiler_params=pltpu.CompilerParams(collective_id=0, has_side_effects=True, vmem_limit_bytes=4 * 2**20),
    )(*shards)

WIDTH = 1024
HEADS = 8
KERNEL = 9
WINDOW = 128
HEAD_DIM = 128
QUARTER = 20
SPAN = 41
NORM_EPSILON = 1e-05
VMEM_LIMIT = 60 * 2**20
BF16 = jnp.bfloat16
F32 = jnp.float32


def dot(a, b):
    return jnp.dot(a, b, preferred_element_type=F32)


def segments(positions, bounds, limit):
    counted = sum((positions >= b).astype(jnp.int32) for b in bounds)
    return jnp.where((positions >= 0) & (positions < limit), counted, -1)


def read_bounds(lengths_ref):
    first = lengths_ref[0, 0]
    second = first + lengths_ref[0, 1]
    return first, second, second + lengths_ref[0, 2]


def normalised(values, gain):
    centred = values - jnp.mean(values, axis=-1, keepdims=True)
    variance = jnp.mean(centred * centred, axis=-1, keepdims=True)
    return centred * lax.rsqrt(variance + NORM_EPSILON) * gain


def norm_rows(source, gain_ref, target, step=64):
    gain = gain_ref[...]

    def body(i, carry):
        rows = pl.ds(pl.multiple_of(i * step, step), step)
        target[rows, :] = normalised(source[rows, :], gain).astype(target.dtype)
        return carry

    lax.fori_loop(0, source.shape[0] // step, body, 0)


def conv_kernel(
    lengths_ref, edge_ref, mel_ref, w_first_ref, w2_ref, wp_hbm, gain_ref, wq_hbm,
    hidden_ref, mixed_ref,
    melf, x_ref, band, w2s, even, odd, sub, wp, wq, normed, sems,
):
    tokens = mel_ref.shape[0] // 4
    channels = w_first_ref.shape[-1]
    frames_all = mel_ref.shape[0] * lax.axis_size("tm")
    copy_p = pltpu.make_async_copy(wp_hbm, wp, sems.at[0])
    copy_q = pltpu.make_async_copy(wq_hbm, wq, sems.at[1])
    copy_p.start()
    copy_q.start()
    bounds = read_bounds(lengths_ref)

    melf[0:8, :] = edge_ref[...].astype(F32)
    melf[8:, :] = mel_ref[...].astype(F32)
    bins = mel_ref.shape[1]
    base = 4 * tokens * lax.axis_index("tm")
    here = base + 4 * lax.broadcasted_iota(jnp.int32, (tokens, bins), 0)
    seg_here = segments(here, bounds, frames_all)

    def frame(d):
        return melf[pl.ds(8 + d, tokens, stride=4), :]

    def same(d):
        return (segments(here + d, bounds, frames_all) == seg_here).astype(F32)

    low2, up2 = same(-2), same(2)
    rows = (
        (frame(-3) * same(-3), frame(-2) * low2, frame(-1) * low2),
        (frame(-1) * same(-1), frame(0), frame(1) * same(1)),
        (frame(1) * up2, frame(2) * up2, frame(3) * same(3)),
    )
    bin_at = lax.broadcasted_iota(jnp.int32, (bins, 256), 0)
    place = lax.broadcasted_iota(jnp.int32, (bins, 256), 1)
    half, within = place // 128, place % 128
    for v in range(3):
        total = jnp.zeros((tokens, 256), F32)
        for a in range(3):
            column = within - SPAN * a
            chosen = (column >= 0) & (column < SPAN) & (bin_at == 40 * half - 1 + column)
            total = total + dot(rows[v][a].astype(BF16), chosen.astype(F32).astype(BF16))
        total = total.astype(BF16)
        for h in range(2):
            piece = total[:, 128 * h : 128 * (h + 1)]
            x_ref[h, v * tokens : (v + 1) * tokens, 0:128] = piece
            x_ref[h, v * tokens : (v + 1) * tokens, 128:256] = piece

    row_at = lax.broadcasted_iota(jnp.int32, (256, channels), 0)
    low_part, r = row_at // 128, row_at % 128
    at = r // SPAN
    column = r - SPAN * at
    spread = []
    for b in range(3):
        value = jnp.zeros((256, channels), F32)
        for a in range(3):
            w = w_first_ref[a, b : b + 1, :]
            top = w.astype(BF16).astype(F32)
            value = jnp.where(at == a, jnp.where(low_part == 0, top, w - top), value)
        spread.append(value)

    def make_band(f, carry):
        value = jnp.zeros((256, channels), F32)
        for b in range(3):
            value = jnp.where(column == 2 * f + b, spread[b], value)
        band[f] = value.astype(BF16)
        return carry

    lax.fori_loop(0, QUARTER, make_band, 0)

    for a in range(3):
        for b in range(3):
            start = (3 * a + b) * channels
            w2s[b, a * channels : (a + 1) * channels, :] = w2_ref[start : start + channels, :]

    odd[1] = jnp.zeros(odd.shape[1:], BF16)

    def conv_step(f2, carry):
        h = f2 // 10
        f = 2 * f2 - 20 * h
        slot = f2 % 2
        for part, target in ((0, even), (1, odd.at[slot])):
            for v in range(3):
                made = dot(x_ref[h, v * tokens : (v + 1) * tokens, :], band[f + part])
                target[:, v * channels : (v + 1) * channels] = jnp.maximum(made, 0.0).astype(BF16)
        total = dot(odd[1 - slot], w2s[0]) + dot(even[...], w2s[1]) + dot(odd[slot], w2s[2])
        columns = pl.ds(pl.multiple_of(f2 * channels, channels), channels)
        sub[:, columns] = jnp.maximum(total, 0.0).astype(BF16)
        return carry

    lax.fori_loop(0, QUARTER, conv_step, 0)
    copy_p.wait()

    def proj_step(n, carry):
        columns = pl.ds(pl.multiple_of(n * 256, 256), 256)
        hidden_ref[:, columns] = dot(sub[...], wp[:, columns])
        return carry

    lax.fori_loop(0, WIDTH // 256, proj_step, 0)
    norm_rows(hidden_ref, gain_ref, normed)
    copy_q.wait()

    def mix_step(n, carry):
        columns = pl.ds(pl.multiple_of(n * 256, 256), 256)
        mixed_ref[:, columns] = dot(normed[...], wq[:, columns]).astype(BF16)
        return carry

    lax.fori_loop(0, 3 * WIDTH // 256, mix_step, 0)


def attend_kernel(
    lengths_ref, mixed_ref, low_ref, high_ref, hidden_ref, wo_ref, gain_ref, wi_ref,
    attended_ref, gated_ref,
    keyval, bias, context, normed,
):
    tokens = mixed_ref.shape[0]
    limit = 4 * tokens * lax.axis_size("tm")
    bounds = read_bounds(lengths_ref)
    base = tokens * lax.axis_index("tm")
    keyval[0:WINDOW, :] = low_ref[...]
    keyval[WINDOW : WINDOW + tokens, :] = mixed_ref[:, WIDTH:]
    keyval[WINDOW + tokens :, :] = high_ref[...]
    reach = 3 * WINDOW
    q_at = lax.broadcasted_iota(jnp.int32, (WINDOW, 1), 0)
    k_at = lax.broadcasted_iota(jnp.int32, (1, reach), 1) - WINDOW
    near = jnp.abs(k_at - q_at) <= WINDOW

    def block_step(block, carry):
        start = pl.multiple_of(block * WINDOW, WINDOW)
        q_rows, k_rows = pl.ds(start, WINDOW), pl.ds(start, reach)
        q_seg = segments(4 * (base + start + q_at), bounds, limit)
        k_seg = segments(4 * (base + start + k_at), bounds, limit)
        bias[...] = jnp.where(near & (q_seg == k_seg), 0.0, -1e30)
        for head in range(HEADS):
            own = slice(head * HEAD_DIM, (head + 1) * HEAD_DIM)
            values = slice(WIDTH + head * HEAD_DIM, WIDTH + (head + 1) * HEAD_DIM)
            scores = lax.dot_general(
                mixed_ref[q_rows, own], keyval[k_rows, own], (((1,), (1,)), ((), ())),
                preferred_element_type=F32,
            ) * HEAD_DIM ** (-0.5) + bias[...]
            exped = jnp.exp(scores - jnp.max(scores, axis=-1, keepdims=True))
            share = 1.0 / jnp.sum(exped, axis=-1, keepdims=True)
            context[q_rows, own] = dot((exped * share).astype(BF16), keyval[k_rows, values]).astype(BF16)
        return carry

    lax.fori_loop(0, tokens // WINDOW, block_step, 0)

    def out_step(n, carry):
        columns = pl.ds(pl.multiple_of(n * 256, 256), 256)
        attended_ref[:, columns] = hidden_ref[:, columns] + dot(context[...], wo_ref[:, columns])
        return carry

    lax.fori_loop(0, WIDTH // 256, out_step, 0)
    norm_rows(attended_ref, gain_ref, normed)

    def gate_step(n, carry):
        start = pl.multiple_of(n * 256, 256)
        value = dot(normed[...], wi_ref[:, pl.ds(start, 256)])
        gate = dot(normed[...], wi_ref[:, pl.ds(WIDTH + start, 256)])
        gated_ref[:, pl.ds(start, 256)] = (value * jax.nn.sigmoid(gate)).astype(BF16)
        return carry

    lax.fori_loop(0, WIDTH // 256, gate_step, 0)


def depth_kernel(
    lengths_ref, gated_ref, low_ref, high_ref, w_depth_ref, attended_ref, wu_ref, gain_ref,
    out_ref,
    extended, acted, combined,
):
    tokens = gated_ref.shape[0]
    limit = 4 * tokens * lax.axis_size("tm")
    bounds = read_bounds(lengths_ref)
    base = tokens * lax.axis_index("tm")
    extended[0:8, :] = low_ref[...].astype(F32)
    extended[8 : 8 + tokens, :] = gated_ref[...].astype(F32)
    extended[8 + tokens :, :] = high_ref[...].astype(F32)
    block = 64
    reach = KERNEL // 2

    def depth_step(i, carry):
        start = pl.multiple_of(i * block, block)
        position = base + start + lax.broadcasted_iota(jnp.int32, (block, 1), 0)
        own = segments(4 * position, bounds, limit)
        same = [
            (segments(4 * (position + k - reach), bounds, limit) == own).astype(F32)
            for k in range(KERNEL)
        ]
        for n in range(WIDTH // 256):
            columns = slice(n * 256, (n + 1) * 256)
            window = extended[pl.ds(start, block + 16), columns]
            total = jnp.zeros((block, 256), F32)
            for k in range(KERNEL):
                taken = window[4 + k : 4 + k + block]
                total = total + taken * w_depth_ref[k : k + 1, columns] * same[k]
            acted[pl.ds(start, block), columns] = (total * jax.nn.sigmoid(total)).astype(BF16)
        return carry

    lax.fori_loop(0, tokens // block, depth_step, 0)

    def out_step(n, carry):
        columns = pl.ds(pl.multiple_of(n * 256, 256), 256)
        combined[:, columns] = attended_ref[:, columns] + dot(acted[...], wu_ref[:, columns])
        return carry

    lax.fori_loop(0, WIDTH // 256, out_step, 0)
    norm_rows(combined, gain_ref, out_ref)


def along(block, step):
    devices = range(lax.axis_size("tm"))
    return lax.ppermute(block, "tm", [(i, i + step) for i in devices if i + step in devices])


def call(kernel, outs, scratch, specs, *args):
    vmem = pl.BlockSpec(memory_space=pltpu.VMEM)
    return pl.pallas_call(
        kernel,
        out_shape=outs,
        in_specs=[vmem if s is None else pl.BlockSpec(memory_space=s) for s in specs],
        out_specs=[vmem] * len(outs),
        scratch_shapes=scratch,
        compiler_params=pltpu.CompilerParams(vmem_limit_bytes=VMEM_LIMIT),
    )(*args)


def on_device(
    mel_frames, lengths, w_first, w_second, w_proj, gain_attn, w_qkv, w_out, gain_conv,
    w_point_in, w_depth, w_point_out, gain_out,
):
    mel = mel_frames[0]
    tokens = mel.shape[0] // 4
    bins = mel.shape[1]
    channels = w_first.shape[-1]
    parts = gather_all((w_second, w_proj, w_qkv, w_out, w_point_in, w_point_out))
    w2, wp, wq, wo, wi, wu = [
        part.reshape(128 * part.shape[4], part.shape[5]) for part in parts
    ]
    gain_attn, gain_conv, gain_out = (g[None] for g in (gain_attn, gain_conv, gain_out))
    edge = along(mel[-8:], 1)
    hidden, mixed = call(
        conv_kernel,
        [jax.ShapeDtypeStruct((tokens, WIDTH), F32), jax.ShapeDtypeStruct((tokens, 3 * WIDTH), BF16)],
        [
            pltpu.VMEM((4 * tokens + 8, bins), F32),
            pltpu.VMEM((2, 3 * tokens, 256), BF16),
            pltpu.VMEM((QUARTER, 256, channels), BF16),
            pltpu.VMEM((3, 3 * channels, channels), BF16),
            pltpu.VMEM((tokens, 3 * channels), BF16),
            pltpu.VMEM((2, tokens, 3 * channels), BF16),
            pltpu.VMEM((tokens, QUARTER * channels), BF16),
            pltpu.VMEM(wp.shape, BF16),
            pltpu.VMEM(wq.shape, BF16),
            pltpu.VMEM((tokens, WIDTH), BF16),
            pltpu.SemaphoreType.DMA((2,)),
        ],
        [pltpu.SMEM, None, None, None, None, pl.ANY, None, pl.ANY],
        lengths, edge, mel, w_first, w2, wp, gain_attn, wq,
    )
    low = along(mixed[tokens - WINDOW :, WIDTH:], 1)
    high = along(mixed[:WINDOW, WIDTH:], -1)
    attended, gated = call(
        attend_kernel,
        [jax.ShapeDtypeStruct((tokens, WIDTH), F32), jax.ShapeDtypeStruct((tokens, WIDTH), BF16)],
        [
            pltpu.VMEM((tokens + 2 * WINDOW, 2 * WIDTH), BF16),
            pltpu.VMEM((WINDOW, 3 * WINDOW), F32),
            pltpu.VMEM((tokens, WIDTH), BF16),
            pltpu.VMEM((tokens, WIDTH), BF16),
        ],
        [pltpu.SMEM] + [None] * 7,
        lengths, mixed, low, high, hidden, wo, gain_conv, wi,
    )
    low = along(gated[tokens - 8 :], 1)
    high = along(gated[:8], -1)
    (encoded,) = call(
        depth_kernel,
        [jax.ShapeDtypeStruct((tokens, WIDTH), BF16)],
        [
            pltpu.VMEM((tokens + 16, WIDTH), F32),
            pltpu.VMEM((tokens, WIDTH), BF16),
            pltpu.VMEM((tokens, WIDTH), F32),
        ],
        [pltpu.SMEM] + [None] * 7,
        lengths, gated, low, high, w_depth, attended, wu, gain_out,
    )
    return encoded[None]


def solution(mesh):
    weight = P(("rec", "tm"), None)
    placed = (
        P("rec", "tm", None), P("rec", None), P(), weight, weight, P(), weight, weight, P(),
        weight, P(), weight, P(),
    )
    return jax.shard_map(
        on_device, mesh=mesh, in_specs=placed, out_specs=P("rec", "tm", None), check_vma=False
    )
```

time: 886 us -> 201 us (0.23)
  the two profiles are of different devices: /device:TPU:0 before, /device:TPU:2 now
where the time goes in v1:
time: 201 us
  Pallas kernels  150 us (75%)
  local copies, waits for them, and re-layouts  22.2 us (11%)
  waiting for transfers between devices  15.4 us (8%)
  starting transfers between devices  12.7 us (6%)
    pallas_call x3, Pallas kernels, call(): pl.pallas_call(kernel, out_shape=outs, in_specs=[vmem if s is None else p...  85.8 us
    pallas_call x1, Pallas kernels, gather_all(): pl.pallas_call(gather_kernel, out_shape=[jax.ShapeDtypeStruct((4, 4, 4, 2...  64.5 us
    unnamed x35, local copies, waits for them, and re-layouts  19 us
    ppermute x5, waiting for transfers between devices, along(): lax.ppermute(block, 'tm', [(i, i + step) for i in devices if i + step in...  15.4 us
    ppermute x5, starting transfers between devices, along(): lax.ppermute(block, 'tm', [(i, i + step) for i in devices if i + step in...  12.7 us
  transfers between devices with their start and end apart: 5, of which 3 were waited for; matrix products, arithmetic and copies ran while one was open for 1% of the time, Pallas kernels for 32%

profile of v1, /device:TPU:2, one launch (start us, length us, event | category | flops | bytes accessed | tf_op | source)
XLA Modules:
  0.0 200.8 jit_solution(17529020584890895491)
XLA Ops:
  0.0 1.2 copy.16
  1.2 0.0 copy-start.11
  1.3 1.9 collective-permute-start
  3.2 0.0 copy-start.5
  3.2 0.9 copy-done.5
  4.1 0.0 copy-start.6
  4.1 0.8 copy-done.6
  4.9 0.0 copy-start.7
  4.9 0.8 copy-done.7
  5.6 0.0 copy-start.8
  5.7 0.7 copy-done.8
  6.4 0.0 copy-start.9
  6.4 0.7 copy-done.9
  7.1 0.0 copy-start.10
  7.1 0.7 copy-done.10
  7.8 64.5 %shard_map.127 = (bf16[4,4,4,2,18,256]{5,4,3,2,1,0:T(8,128)(2,1)S(1)}, bf16[4,4,4,2,40,1024]{5,4,3,2,1,0:T(8,128)(2,1)S(1)}, bf16[4,4,4,2,8,3072]{5,4,3,2,1,0:T(...) custom-call(bf16[18,256]{1,0:T(8,128)(2,1)S(1)} %copy-done.10, ...), custom_call_target="tpu_custom_call" | custom-call | tf_op jit(solution)/shard_map/pallas_call | solution.py:124
  72.3 0.0 copy-start
  72.4 4.0 %copy-done = bf16[4,4,4,2,40,1024]{5,4,3,2,1,0:T(8,128)(2,1)} copy-done((bf16[4,4,4,2,40,1024]{5,4,3,2,1,0:T(8,128)(2,1)}, bf16[4,4,4,2,40,1024]{5,4,3,2,1,0:T(8,128)(2,1)S(1)}, u32[]{:S(2)}) %copy-start) | copy-done | bytes 10485784
  76.4 0.0 copy-start.1
  76.4 2.6 %copy-done.1 = bf16[4,4,4,2,8,3072]{5,4,3,2,1,0:T(8,128)(2,1)} copy-done((bf16[4,4,4,2,8,3072]{5,4,3,2,1,0:T(8,128)(2,1)}, bf16[4,4,4,2,8,3072]{5,4,3,2,1,0:T(8,128)(2,1)S(1)}, u32[]{:S(2)}) %copy-start.1) | copy-done | bytes 6291480
  79.0 0.0 copy-start.2
  79.0 1.9 copy-done.2
  80.9 0.0 copy-start.3
  80.9 1.4 copy-done.3
  82.3 0.0 copy-start.4
  82.3 1.3 copy-done.4
  83.6 1.2 reshape.19.w2_ref
  84.8 0.0 collective-permute-done.edge_ref
  84.8 0.0 copy-start.16
  84.8 0.0 copy-done.11
  84.8 0.5 copy-done.16
  85.4 49.6 %shard_map.128 = (f32[512,1024]{1,0:T(8,128)}, bf16[512,3072]{1,0:T(8,128)(2,1)}) custom-call(s32[1,4]{1,0:T(1,128)} %lengths_ref.5, bf16[8,80]{1,0:T(8,128)(2,1)} %copy-done.16, bf16[2048,80]{1,0:T(8,128)(2,1)} %bitcast.17, f32[3,3,256]{2,1,0:T(4,128)} %w_first_ref.1, bf16[2304,256]{1,0:T(8,128)(2,1)} %reshape.19.w2_ref, bf16[5120,1024]{1,0:T(8,128)(2,1)} %bitcast.12, ...), custom_call_target="tpu_custom_call" | custom-call | tf_op jit(solution)/shard_map/pallas_call | solution.py:398
  134.9 1.3 fusion
  136.2 4.5 %collective-permute-start.2 = (bf16[128,2048]{1,0:T(8,128)(2,1)S(1)}, bf16[128,2048]{1,0:T(8,128)(2,1)S(1)}, u32[]{:S(2)}, u32[]{:S(2)}) collective-permute-start(bf16[128,2048]{1,0:T(8,128)(2,1)S(1)} %get-tuple-element.25), channel_id=1, source_target_pairs={{1,0},{2,1},{3,2},{4,3},{5,4},{6,5},{7,6},{8,7},{9,8},{10,9},{11,1... | collective-permute-start | bytes 1572872 | tf_op jit(solution)/shard_map/ppermute | solution.py:393
  140.7 1.9 collective-permute-start.1
  142.7 4.7 %collective-permute-done.2.high_ref = bf16[128,2048]{1,0:T(8,128)(2,1)S(1)} collective-permute-done((bf16[128,2048]{1,0:T(8,128)(2,1)S(1)}, bf16[128,2048]{1,0:T(8,128)(2,1)S(1)}, u32[]{:S(2)}, u32[]{:S(2)}) %collective-permute-start.2) | collective-permute-done | bytes 524320 | tf_op jit(solution)/shard_map/ppermute | solution.py:393
  147.4 0.0 copy-start.12
  147.4 5.9 %collective-permute-done.1.low_ref = bf16[128,2048]{1,0:T(8,128)(2,1)S(1)} collective-permute-done((bf16[128,2048]{1,0:T(8,128)(2,1)S(1)}, bf16[128,2048]{1,0:T(8,128)(2,1)S(1)}, u32[]{:S(2)}, u32[]{:S(2)}) %collective-permute-start.1) | collective-permute-done | bytes 524320 | tf_op jit(solution)/shard_map/ppermute | solution.py:393
  153.4 0.0 copy-start.13
  153.4 0.0 copy-done.12
  153.4 0.8 copy-done.13
  154.1 23.7 %shard_map.129 = (f32[512,1024]{1,0:T(8,128)}, bf16[512,1024]{1,0:T(8,128)(2,1)}) custom-call(s32[1,4]{1,0:T(1,128)} %lengths_ref.5, bf16[512,3072]{1,0:T(8,128)(2,1)} %get-tuple-element.18.mixed_ref, bf16[128,2048]{1,0:T(8,128)(2,1)} %copy-done.13, bf16[128,2048]{1,0:T(8,128)(2,1)} %copy-done.12, f32[512,1024]{1,0:T(8,128)} %get-tuple-element.19.hidden_ref, ...), custom_call_target="tpu_custom_call" | custom-call | tf_op jit(solution)/shard_map/pallas_call | solution.py:398
  177.9 0.7 fusion.1
  178.6 1.9 collective-permute-start.4
  180.5 2.4 %collective-permute-start.3 = (bf16[8,1024]{1,0:T(8,128)(2,1)S(1)}, bf16[8,1024]{1,0:T(8,128)(2,1)S(1)}, u32[]{:S(2)}, u32[]{:S(2)}) collective-permute-start(bf16[8,1024]{1,0:T(8,128)(2,1)S(1)} %get-tuple-element.28), channel_id=1, source_target_pairs={{0,1},{1,2},{2,3},{3,4},{4,5},{5,6},{6,7},{7,8},{8,9},{9,10},{10,1... | collective-permute-start | bytes 49160 | tf_op jit(solution)/shard_map/ppermute | solution.py:393
  182.9 0.0 collective-permute-done.4.high_ref
  183.0 0.0 copy-start.14
  183.0 4.7 %collective-permute-done.3.low_ref = bf16[8,1024]{1,0:T(8,128)(2,1)S(1)} collective-permute-done((bf16[8,1024]{1,0:T(8,128)(2,1)S(1)}, bf16[8,1024]{1,0:T(8,128)(2,1)S(1)}, u32[]{:S(2)}, u32[]{:S(2)}) %collective-permute-start.3) | collective-permute-done | bytes 16416 | tf_op jit(solution)/shard_map/ppermute | solution.py:393
  187.7 0.0 copy-start.15
  187.7 0.0 copy-done.14
  187.7 0.6 copy-done.15
  188.3 12.5 %shard_map.130 = bf16[512,1024]{1,0:T(8,128)(2,1)} custom-call(s32[1,4]{1,0:T(1,128)} %lengths_ref.5, bf16[512,1024]{1,0:T(8,128)(2,1)} %get-tuple-element.22.gated_ref, bf16[8,1024]{1,0:T(8,128)(2,1)} %copy-done.15, bf16[8,1024]{1,0:T(8,128)(2,1)} %copy-done.14, f32[9,1024]{1,0:T(8,128)} %w_depth_ref.1, f32[512,1024]{1,0:T(8,128)} %get-tuple-element.23.attended_ref, ...), custom_call_target="tpu_custom_call" | custom-call | tf_op jit(solution)/shard_map/pallas_call | solution.py:398
  (1 shorter events, 0.0 us)
Async XLA Ops:
  1.2 83.6 %copy-start.11 = (bf16[1,2048,80]{2,1,0:T(8,128)(2,1)}, bf16[1,2048,80]{2,1,0:T(8,128)(2,1)S(1)}, u32[]{:S(2)}) copy-start(bf16[1,2048,80]{2,1,0:T(8,128)(2,1)S(1)} %copy.16) | copy-start | bytes 983044
  1.3 83.6 %collective-permute-start = (bf16[8,80]{1,0:T(8,128)(2,1)S(1)}, bf16[8,80]{1,0:T(8,128)(2,1)S(1)}, u32[]{:S(2)}, u32[]{:S(2)}) collective-permute-start(bf16[8,80]{1,0:T(8,128)(2,1)S(1)} %slice_bitcast_fusion), channel_id=1, source_target_pairs={{0,1},{1,2},{2,3},{3,4},{4,5},{5,6},{6,7},{7,8},{8,9},{9,10},{10,1... | collective-permute-start | bytes 3848 | tf_op jit(solution)/shard_map/ppermute | solution.py:393
  3.2 0.9 copy-start.5
  4.1 0.8 copy-start.6
  4.9 0.8 copy-start.7
  5.6 0.7 copy-start.8
  6.4 0.7 copy-start.9
  7.1 0.7 copy-start.10
  72.3 4.0 %copy-start = (bf16[4,4,4,2,40,1024]{5,4,3,2,1,0:T(8,128)(2,1)}, bf16[4,4,4,2,40,1024]{5,4,3,2,1,0:T(8,128)(2,1)S(1)}, u32[]{:S(2)}) copy-start(bf16[4,4,4,2,40,1024]{5,4,3,2,1,0:T(8,128)(2,1)S(1)} %get-tuple-element.16) | copy-start | bytes 31457284
  76.4 2.6 %copy-start.1 = (bf16[4,4,4,2,8,3072]{5,4,3,2,1,0:T(8,128)(2,1)}, bf16[4,4,4,2,8,3072]{5,4,3,2,1,0:T(8,128)(2,1)S(1)}, u32[]{:S(2)}) copy-start(bf16[4,4,4,2,8,3072]{5,4,3,2,1,0:T(8,128)(2,1)S(1)} %get-tuple-element.17) | copy-start | bytes 18874372
  79.0 1.9 copy-start.2
  80.9 1.4 copy-start.3
  82.3 1.3 copy-start.4
  84.8 0.5 copy-start.16
  136.2 11.2 %collective-permute-start.2 = (bf16[128,2048]{1,0:T(8,128)(2,1)S(1)}, bf16[128,2048]{1,0:T(8,128)(2,1)S(1)}, u32[]{:S(2)}, u32[]{:S(2)}) collective-permute-start(bf16[128,2048]{1,0:T(8,128)(2,1)S(1)} %get-tuple-element.25), channel_id=1, source_target_pairs={{1,0},{2,1},{3,2},{4,3},{5,4},{6,5},{7,6},{8,7},{9,8},{10,9},{11,1... | collective-permute-start | bytes 1572872 | tf_op jit(solution)/shard_map/ppermute | solution.py:393
  140.7 12.6 %collective-permute-start.1 = (bf16[128,2048]{1,0:T(8,128)(2,1)S(1)}, bf16[128,2048]{1,0:T(8,128)(2,1)S(1)}, u32[]{:S(2)}, u32[]{:S(2)}) collective-permute-start(bf16[128,2048]{1,0:T(8,128)(2,1)S(1)} %get-tuple-element.26), channel_id=1, source_target_pairs={{0,1},{1,2},{2,3},{3,4},{4,5},{5,6},{6,7},{7,8},{8,9},{9,10},{10,1... | collective-permute-start | bytes 1572872 | tf_op jit(solution)/shard_map/ppermute | solution.py:393
  147.4 5.9 %copy-start.12 = (bf16[128,2048]{1,0:T(8,128)(2,1)}, bf16[128,2048]{1,0:T(8,128)(2,1)S(1)}, u32[]{:S(2)}) copy-start(bf16[128,2048]{1,0:T(8,128)(2,1)S(1)} %collective-permute-done.2.high_ref) | copy-start | bytes 1572868
  153.4 0.8 copy-start.13
  178.6 4.3 %collective-permute-start.4 = (bf16[8,1024]{1,0:T(8,128)(2,1)S(1)}, bf16[8,1024]{1,0:T(8,128)(2,1)S(1)}, u32[]{:S(2)}, u32[]{:S(2)}) collective-permute-start(bf16[8,1024]{1,0:T(8,128)(2,1)S(1)} %get-tuple-element.27), channel_id=1, source_target_pairs={{1,0},{2,1},{3,2},{4,3},{5,4},{6,5},{7,6},{8,7},{9,8},{10,9},{11,1... | collective-permute-start | bytes 49160 | tf_op jit(solution)/shard_map/ppermute | solution.py:393
  180.5 7.2 %collective-permute-start.3 = (bf16[8,1024]{1,0:T(8,128)(2,1)S(1)}, bf16[8,1024]{1,0:T(8,128)(2,1)S(1)}, u32[]{:S(2)}, u32[]{:S(2)}) collective-permute-start(bf16[8,1024]{1,0:T(8,128)(2,1)S(1)} %get-tuple-element.28), channel_id=1, source_target_pairs={{0,1},{1,2},{2,3},{3,4},{4,5},{5,6},{6,7},{7,8},{8,9},{9,10},{10,1... | collective-permute-start | bytes 49160 | tf_op jit(solution)/shard_map/ppermute | solution.py:393
  183.0 4.7 %copy-start.14 = (bf16[8,1024]{1,0:T(8,128)(2,1)}, bf16[8,1024]{1,0:T(8,128)(2,1)S(1)}, u32[]{:S(2)}) copy-start(bf16[8,1024]{1,0:T(8,128)(2,1)S(1)} %collective-permute-done.4.high_ref) | copy-start | bytes 49156
  187.7 0.6 copy-start.15

commit v2 on v0

v2 whole, which is shorter than its diff:
```python
import jax
import jax.numpy as jnp
from jax import lax
from jax.experimental import pallas as pl
from jax.experimental.pallas import tpu as pltpu
from jax.sharding import PartitionSpec as P

WIDTH = 1024
HEADS = 8
KERNEL = 9
WINDOW = 128
HEAD_DIM = 128
QUARTER = 20
SPAN = 41
NORM_EPSILON = 1e-05
VMEM_LIMIT = 62 * 2**20
BF16 = jnp.bfloat16
F32 = jnp.float32
MESH = pl.DeviceIdType.MESH

ORDERS = (("x", "y", "z"), ("y", "z", "x"), ("z", "x", "y"))
CHUNKS = (
    (0, 0, 256, 0),
    (1, 0, 256, 0), (1, 256, 384, 1), (1, 640, 384, 2),
    (2, 0, 1024, 0), (2, 1024, 1024, 1), (2, 2048, 1024, 2),
    (3, 0, 1024, 0), (4, 0, 384, 0), (5, 0, 1024, 1), (4, 384, 384, 1), (4, 768, 1280, 2),
)
PHASES = ((0,), (1, 2, 3), (4, 5, 6), (7, 8, 9, 10, 11))
LOOP_STEPS = {
    0: ((1, 3),), 1: ((2, 2),), 2: ((1, 4),), 3: ((3, 1),), 4: ((2, 3),), 6: ((2, 4), (3, 2)),
    7: ((1, 5),), 9: ((3, 3),), 11: ((1, 6), (3, 4)), 12: ((2, 5),), 14: ((1, 7),), 16: ((2, 6),),
    17: ((3, 5),), 19: ((2, 7),),
}
SLOTS = 15


def dot(a, b):
    return jnp.dot(a, b, preferred_element_type=F32)


def segments(positions, bounds, limit):
    counted = sum((positions >= b).astype(jnp.int32) for b in bounds)
    return jnp.where((positions >= 0) & (positions < limit), counted, -1)


def normalised(values, gain):
    centred = values - jnp.mean(values, axis=-1, keepdims=True)
    variance = jnp.mean(centred * centred, axis=-1, keepdims=True)
    return centred * lax.rsqrt(variance + NORM_EPSILON) * gain


def norm_rows(source, gain_ref, target, step=64):
    gain = gain_ref[...]

    def body(i, carry):
        rows = pl.ds(pl.multiple_of(i * step, step), step)
        target[rows, :] = normalised(source[rows, :], gain).astype(target.dtype)
        return carry

    lax.fori_loop(0, source.shape[0] // step, body, 0)


def over_columns(count, body, first=0):
    def step(n, carry):
        body(pl.multiple_of(n * 256, 256))
        return carry

    lax.fori_loop(first, count, step, 0)


class Gather:
    def __init__(self, shards, wholes, send_sems, recv_sems):
        self.shards, self.wholes = shards, wholes
        self.send_sems, self.recv_sems = send_sems, recv_sems
        tm = lax.axis_index("tm")
        self.here = {"z": lax.axis_index("rec"), "x": tm // 8, "y": (tm // 2) % 4}
        self.core = tm % 2
        self.near = {
            (axis, step): {**self.here, axis: (self.here[axis] + step) % 4}
            for axis in ("x", "y", "z")
            for step in (1, 2, 3)
        }

    def device(self, position, core):
        return {"rec": position["z"], "tm": position["x"] * 8 + position["y"] * 2 + core}

    def peers(self):
        chips = [self.device(position, self.core) for position in self.near.values()]
        return chips + [self.device(self.here, 1 - self.core)]

    def view(self, chunk, stage, position, half=None):
        array, column, columns, order = CHUNKS[chunk]
        free = ORDERS[order][: stage - 1]
        index = []
        for axis in ("z", "x", "y"):
            if axis not in free:
                index.append(position[axis])
            elif half is not None and axis == free[0]:
                index.append(pl.ds(2 * half, 2))
            else:
                index.append(slice(None))
        return self.wholes[array].at[tuple(index) + (self.core, slice(None), pl.ds(column, columns))]

    def copy(self, chunk, slot):
        array, column, columns, order = CHUNKS[chunk]
        axes = ORDERS[order]
        target = None
        if slot < 3:
            target = self.near[axes[0], (1, 3, 2)[slot]]
            source = self.shards[array].at[:, pl.ds(column, columns)]
            place = self.view(chunk, 1, self.here)
        elif slot < 11:
            stage = 2 if slot < 7 else 3
            axis = axes[stage - 1]
            at = (slot - 3) % 4
            target = self.near[axis, (1, 3, 1, 3)[at]]
            if at < 2:
                source = self.view(chunk, stage, self.here)
            else:
                source = self.view(chunk, stage, self.near[axis, (3, 1)[at - 2]], at - 2)
            place = source
        else:
            axis = axes[2]
            at = slot - 11
            source = self.view(chunk, 3, self.here if at == 0 else self.near[axis, (3, 1, 2)[at - 1]])
            place = source
        where = self.device(self.here, 1 - self.core) if target is None else self.device(target, self.core)
        return pltpu.make_async_remote_copy(
            src_ref=source, dst_ref=place, send_sem=self.send_sems.at[chunk, slot],
            recv_sem=self.recv_sems.at[chunk, slot], device_id=where, device_id_type=MESH,
        )

    def step(self, phase, number):
        awaited = ((), (0, 1, 2), (3, 4), (5, 6), (7, 8), (9, 10), (11, 12, 13, 14))[number - 1]
        started = ((0, 1, 2), (3, 4), (5, 6), (7, 8, 11), (9, 10, 12, 13), (14,), ())[number - 1]
        for chunk in PHASES[phase]:
            for slot in awaited:
                self.copy(chunk, slot).wait_recv()
            for slot in started:
                self.copy(chunk, slot).start()

    def finish(self):
        for chunk in range(len(CHUNKS)):
            for slot in range(SLOTS):
                self.copy(chunk, slot).wait_send()


def block_kernel(
    lengths_ref, mel_ref, w_first_ref, gain_attn_ref, gain_conv_ref, w_depth_ref, gain_out_ref,
    ws_shard, wp_shard, wq_shard, wo_shard, wi_shard, wu_shard,
    out_ref,
    edge, melf, x_ref, band, ws, wp, wq, wo, wi, wu, w2, w2s, even, odd, sub,
    hidden, normed, query, keyval, bias, context, extended,
    send_sems, recv_sems, own_sems, halo_send, halo_recv,
):
    tokens = mel_ref.shape[0] // 4
    channels = w_first_ref.shape[-1]
    bins = mel_ref.shape[1]
    tm = lax.axis_index("tm")
    count = lax.axis_size("tm")
    rec = lax.axis_index("rec")
    frames_all = mel_ref.shape[0] * count
    shards = (ws_shard, wp_shard, wq_shard, wo_shard, wi_shard, wu_shard)
    wholes = (ws, wp, wq, wo, wi, wu)
    gather = Gather(shards, wholes, send_sems, recv_sems)
    after = {"rec": rec, "tm": (tm + 1) % count}
    before = {"rec": rec, "tm": (tm + count - 1) % count}

    barrier = pltpu.get_barrier_semaphore()
    greeted = gather.peers() + [after, before]
    for device in greeted:
        pl.semaphore_signal(barrier, inc=1, device_id=device, device_id_type=MESH)

    def own_copy(array):
        here = gather.here
        place = wholes[array].at[here["z"], here["x"], here["y"], gather.core]
        return pltpu.make_async_copy(shards[array], place, own_sems.at[array])

    for array in range(6):
        own_copy(array).start()
    pl.semaphore_wait(barrier, len(greeted))

    def pass_on(source, place, device, number):
        return pltpu.make_async_remote_copy(
            src_ref=source, dst_ref=place, send_sem=halo_send.at[number],
            recv_sem=halo_recv.at[number], device_id=device, device_id_type=MESH,
        )

    def weight(array, start):
        whole = wholes[array]
        value = whole[:, :, :, :, :, pl.ds(start, 256)]
        return value.reshape(128 * whole.shape[4], 256)

    gather.step(0, 1)
    edge_copy = pass_on(mel_ref.at[pl.ds(4 * tokens - 8, 8), :], edge, after, 0)
    edge_copy.start()
    gather.step(1, 1)
    gather.step(2, 1)
    for array in range(6):
        own_copy(array).wait()

    first = lengths_ref[0, 0]
    second = first + lengths_ref[0, 1]
    bounds = (first, second, second + lengths_ref[0, 2])

    row_at = lax.broadcasted_iota(jnp.int32, (256, channels), 0)
    low_part, r = row_at // 128, row_at % 128
    at = r // SPAN
    column = r - SPAN * at
    spread = []
    for b in range(3):
        value = jnp.zeros((256, channels), F32)
        for a in range(3):
            w = w_first_ref[a, b : b + 1, :]
            top = w.astype(BF16).astype(F32)
            value = jnp.where(at == a, jnp.where(low_part == 0, top, w - top), value)
        spread.append(value)

    gather.step(0, 2)

    def make_band(f, carry):
        value = jnp.zeros((256, channels), F32)
        for b in range(3):
            value = jnp.where(column == 2 * f + b, spread[b], value)
        band[f] = value.astype(BF16)
        return carry

    lax.fori_loop(0, QUARTER // 2, make_band, 0)
    gather.step(0, 3)
    lax.fori_loop(QUARTER // 2, QUARTER, make_band, 0)
    gather.step(0, 4)
    edge_copy.wait_recv()

    melf[0:8, :] = edge[...].astype(F32)
    melf[8:, :] = mel_ref[...].astype(F32)
    frame_at = 4 * tokens * tm + 4 * lax.broadcasted_iota(jnp.int32, (tokens, bins), 0)
    seg_here = segments(frame_at, bounds, frames_all)

    def frame(d):
        return melf[pl.ds(8 + d, tokens, stride=4), :]

    def same(d):
        return (segments(frame_at + d, bounds, frames_all) == seg_here).astype(F32)

    low2, up2 = same(-2), same(2)
    rows = (
        (frame(-3) * same(-3), frame(-2) * low2, frame(-1) * low2),
        (frame(-1) * same(-1), frame(0), frame(1) * same(1)),
        (frame(1) * up2, frame(2) * up2, frame(3) * same(3)),
    )
    bin_at = lax.broadcasted_iota(jnp.int32, (bins, 256), 0)
    place = lax.broadcasted_iota(jnp.int32, (bins, 256), 1)
    half, within = place // 128, place % 128
    for v in range(3):
        total = jnp.zeros((tokens, 256), F32)
        for a in range(3):
            taken = within - SPAN * a
            chosen = (taken >= 0) & (taken < SPAN) & (bin_at == 40 * half - 1 + taken)
            total = total + dot(rows[v][a].astype(BF16), chosen.astype(F32).astype(BF16))
        total = total.astype(BF16)
        for h in range(2):
            piece = total[:, 128 * h : 128 * (h + 1)]
            x_ref[h, v * tokens : (v + 1) * tokens, 0:128] = piece
            x_ref[h, v * tokens : (v + 1) * tokens, 128:256] = piece
        if v == 0:
            gather.step(0, 5)
        if v == 1:
            gather.step(0, 6)

    gather.step(1, 2)
    gather.step(0, 7)
    depth = ws.shape[4]

    def unpack(i, carry):
        group = w2.at[pl.ds(pl.multiple_of(8 * depth * i, 16), 8 * depth), :]
        for s in range(8):
            group[s * depth : (s + 1) * depth, :] = ws[i // 4, i % 4, s // 2, s % 2]
        return carry

    lax.fori_loop(0, 16, unpack, 0)
    for a in range(3):
        for b in range(3):
            start = (3 * a + b) * channels
            w2s[b, a * channels : (a + 1) * channels, :] = w2[start : start + channels, :]

    odd[1] = jnp.zeros(odd.shape[1:], BF16)

    def conv_step(f2, carry):
        for number, pairs in LOOP_STEPS.items():

            @pl.when(f2 == number)
            def _():
                for phase, step in pairs:
                    gather.step(phase, step)

        h = f2 // 10
        f = 2 * f2 - 20 * h
        slot = f2 % 2
        for part, target in ((0, even), (1, odd.at[slot])):
            for v in range(3):
                made = dot(x_ref[h, v * tokens : (v + 1) * tokens, :], band[f + part])
                target[:, v * channels : (v + 1) * channels] = jnp.maximum(made, 0.0).astype(BF16)
        total = dot(odd[1 - slot], w2s[0]) + dot(even[...], w2s[1]) + dot(odd[slot], w2s[2])
        columns = pl.ds(pl.multiple_of(f2 * channels, channels), channels)
        sub[:, columns] = jnp.maximum(total, 0.0).astype(BF16)
        return carry

    lax.fori_loop(0, QUARTER, conv_step, 0)

    def project(start):
        columns = pl.ds(start, 256)
        hidden[:, columns] = dot(sub[...], weight(1, start))

    over_columns(2, project)
    gather.step(3, 6)
    over_columns(4, project, 2)
    norm_rows(hidden, gain_attn_ref, normed)

    def mix_keyval(start):
        keyval[WINDOW : WINDOW + tokens, pl.ds(start, 256)] = dot(
            normed[...], weight(2, WIDTH + start)
        ).astype(BF16)

    over_columns(2 * WIDTH // 256, mix_keyval)
    halos = (
        pass_on(keyval.at[pl.ds(tokens, WINDOW), :], keyval.at[pl.ds(0, WINDOW), :], after, 1),
        pass_on(
            keyval.at[pl.ds(WINDOW, WINDOW), :], keyval.at[pl.ds(WINDOW + tokens, WINDOW), :], before, 2
        ),
    )
    for copy in halos:
        copy.start()
    gather.step(3, 7)

    def mix_query(start):
        query[:, pl.ds(start, 256)] = dot(normed[...], weight(2, start)).astype(BF16)

    over_columns(WIDTH // 256, mix_query)

    base = tokens * tm
    reach = 3 * WINDOW
    q_at = lax.broadcasted_iota(jnp.int32, (WINDOW, 1), 0)
    k_at = lax.broadcasted_iota(jnp.int32, (1, reach), 1) - WINDOW
    near = jnp.abs(k_at - q_at) <= WINDOW
    blocks = tokens // WINDOW

    def attend(i, carry):
        block = (i + 1) % blocks

        @pl.when(i == blocks - 2)
        def _():
            for copy in halos:
                copy.wait_recv()

        start = pl.multiple_of(block * WINDOW, WINDOW)
        q_rows, k_rows = pl.ds(start, WINDOW), pl.ds(start, reach)
        q_seg = segments(4 * (base + start + q_at), bounds, frames_all)
        k_seg = segments(4 * (base + start + k_at), bounds, frames_all)
        bias[...] = jnp.where(near & (q_seg == k_seg), 0.0, -1e30)
        for head in range(HEADS):
            own = slice(head * HEAD_DIM, (head + 1) * HEAD_DIM)
            values = slice(WIDTH + head * HEAD_DIM, WIDTH + (head + 1) * HEAD_DIM)
            scores = lax.dot_general(
                query[q_rows, own], keyval[k_rows, own], (((1,), (1,)), ((), ())),
                preferred_element_type=F32,
            ) * HEAD_DIM ** (-0.5) + bias[...]
            exped = jnp.exp(scores - jnp.max(scores, axis=-1, keepdims=True))
            share = 1.0 / jnp.sum(exped, axis=-1, keepdims=True)
            context[q_rows, own] = dot((exped * share).astype(BF16), keyval[k_rows, values]).astype(BF16)
        return carry

    lax.fori_loop(0, blocks, attend, 0)

    def attend_out(start):
        columns = pl.ds(start, 256)
        hidden[:, columns] = hidden[:, columns] + dot(context[...], weight(3, start))

    over_columns(WIDTH // 256, attend_out)
    norm_rows(hidden, gain_conv_ref, normed)

    def gate(start):
        value = dot(normed[...], weight(4, start))
        opening = dot(normed[...], weight(4, WIDTH + start))
        gated = (value * jax.nn.sigmoid(opening)).astype(BF16)
        extended[8 : 8 + tokens, pl.ds(start, 256)] = gated.astype(F32)

    over_columns(WIDTH // 256, gate)
    edges = (
        pass_on(extended.at[pl.ds(tokens, 8), :], extended.at[pl.ds(0, 8), :], after, 3),
        pass_on(extended.at[pl.ds(8, 8), :], extended.at[pl.ds(8 + tokens, 8), :], before, 4),
    )
    for copy in edges:
        copy.start()
    rows_at_once = 64
    groups = tokens // rows_at_once
    reach = KERNEL // 2

    def depth_step(i, carry):
        group = (i + 1) % groups

        @pl.when(i == groups - 2)
        def _():
            for copy in edges:
                copy.wait_recv()

        start = pl.multiple_of(group * rows_at_once, rows_at_once)
        position = base + start + lax.broadcasted_iota(jnp.int32, (rows_at_once, 1), 0)
        own = segments(4 * position, bounds, frames_all)
        kept = [
            (segments(4 * (position + k - reach), bounds, frames_all) == own).astype(F32)
            for k in range(KERNEL)
        ]
        for n in range(WIDTH // 256):
            columns = slice(n * 256, (n + 1) * 256)
            window = extended[pl.ds(start, rows_at_once + 16), columns]
            total = jnp.zeros((rows_at_once, 256), F32)
            for k in range(KERNEL):
                taken = window[4 + k : 4 + k + rows_at_once]
                total = total + taken * w_depth_ref[k : k + 1, columns] * kept[k]
            context[pl.ds(start, rows_at_once), columns] = (total * jax.nn.sigmoid(total)).astype(BF16)
        return carry

    lax.fori_loop(0, groups, depth_step, 0)

    def point_out(start):
        columns = pl.ds(start, 256)
        hidden[:, columns] = hidden[:, columns] + dot(context[...], weight(5, start))

    over_columns(WIDTH // 256, point_out)
    norm_rows(hidden, gain_out_ref, out_ref)
    gather.finish()
    for copy in (edge_copy,) + halos + edges:
        copy.wait_send()


def on_device(
    mel_frames, lengths, w_first, w_second, w_proj, gain_attn, w_qkv, w_out, gain_conv,
    w_point_in, w_depth, w_point_out, gain_out,
):
    mel = mel_frames[0]
    tokens = mel.shape[0] // 4
    bins = mel.shape[1]
    channels = w_first.shape[-1]
    shards = (w_second, w_proj, w_qkv, w_out, w_point_in, w_point_out)
    vmem = pl.BlockSpec(memory_space=pltpu.VMEM)
    hbm = pl.BlockSpec(memory_space=pl.ANY)
    (encoded,) = pl.pallas_call(
        block_kernel,
        out_shape=[jax.ShapeDtypeStruct((tokens, WIDTH), BF16)],
        in_specs=[pl.BlockSpec(memory_space=pltpu.SMEM)] + [vmem] * 6 + [hbm] * 6,
        out_specs=[vmem],
        scratch_shapes=[
            pltpu.VMEM((8, bins), BF16),
            pltpu.VMEM((4 * tokens + 8, bins), F32),
            pltpu.VMEM((2, 3 * tokens, 256), BF16),
            pltpu.VMEM((QUARTER, 256, channels), BF16),
            *[pltpu.VMEM((4, 4, 4, 2) + s.shape, BF16) for s in shards],
            pltpu.VMEM((9 * channels, channels), BF16),
            pltpu.VMEM((3, 3 * channels, channels), BF16),
            pltpu.VMEM((tokens, 3 * channels), BF16),
            pltpu.VMEM((2, tokens, 3 * channels), BF16),
            pltpu.VMEM((tokens, QUARTER * channels), BF16),
            pltpu.VMEM((tokens, WIDTH), F32),
            pltpu.VMEM((tokens, WIDTH), BF16),
            pltpu.VMEM((tokens, WIDTH), BF16),
            pltpu.VMEM((tokens + 2 * WINDOW, 2 * WIDTH), BF16),
            pltpu.VMEM((WINDOW, 3 * WINDOW), F32),
            pltpu.VMEM((tokens, WIDTH), BF16),
            pltpu.VMEM((tokens + 16, WIDTH), F32),
            pltpu.SemaphoreType.DMA((len(CHUNKS), SLOTS)),
            pltpu.SemaphoreType.DMA((len(CHUNKS), SLOTS)),
            pltpu.SemaphoreType.DMA((6,)),
            pltpu.SemaphoreType.DMA((5,)),
            pltpu.SemaphoreType.DMA((5,)),
        ],
        compiler_params=pltpu.CompilerParams(
            collective_id=0, has_side_effects=True, vmem_limit_bytes=VMEM_LIMIT
        ),
    )(
        lengths, mel, w_first, gain_attn[None], gain_conv[None], w_depth, gain_out[None], *shards
    )
    return encoded[None]


def solution(mesh):
    weight = P(("rec", "tm"), None)
    placed = (
        P("rec", "tm", None), P("rec", None), P(), weight, weight, P(), weight, weight, P(),
        weight, P(), weight, P(),
    )
    return jax.shard_map(
        on_device, mesh=mesh, in_specs=placed, out_specs=P("rec", "tm", None), check_vma=False
    )
```

time: 886 us -> 134 us (0.15); the launches traced: 874 us -> 133 us
  local copies, waits for them, and re-layouts: 458 us -> 4.24 us
  matrix products: 202 us -> 0 us
  Pallas kernels: 0 us -> 129 us
  other arithmetic: 106 us -> 0 us
  waiting for transfers between devices: 66.7 us -> 0 us
  starting transfers between devices: 15.3 us -> 0 us
  between operations: 13.8 us -> 0.01 us
  loops' own time: 12.5 us -> 0 us
    slice x239 -> x0, local copies, waits for them, and re-layouts: 353 us -> none  [the longest x72 284 us: conv_second(): taken[:, step_f:step_f + 2 * quarter - 1:2]]
    dot_general x93 -> x0, matrix products: 202 us -> none  [the longest x72 145 us: conv_second(): jnp.dot(columns, w_second[offset:offset + channels], preferred_element_ty...]
    pallas_call x0 -> x1, Pallas kernels: none -> 129 us  [on_device(): pl.pallas_call(block_kernel, out_shape=[jax.ShapeDtypeStruct((tokens, WID...]
    convert_element_type x27 -> x0, other arithmetic: 62.3 us -> none  [the longest x8 61.5 us: conv_first(): return jnp.maximum(total, 0.0).astype(jnp.bfloat16)]
    all_gather x6 -> x0, waiting for transfers between devices: 60 us -> none  [the longest x1 59.9 us: on_device(): second_full = lax.all_gather(w_second, ('rec', 'tm'), axis=0, tiled=True)]
    reshape x72 -> x0, local copies, waits for them, and re-layouts: 56 us -> none  [conv_second(): taken[:, step_f:step_f + 2 * quarter - 1:2]]
    mul x19 -> x0, other arithmetic: 25.2 us -> none  [the longest x8 23.8 us: conv_second(): taken = taken * same_seg[:, None, None]]
    dynamic_slice x24 -> x0, local copies, waits for them, and re-layouts: 22.5 us -> none  [the longest x16 15.2 us: on_device(): sub = lax.map(sub_block, jnp.arange(block_count, dtype=jnp.int32))]
  transfers between devices with their start and end apart: 11 -> 0, of which waited for: 3 -> 0; matrix products, arithmetic and copies ran while one was open for 87% -> 0% of each run, Pallas kernels for 0% -> 0%
where the time goes in v2:
time: 134 us; the launch traced here: 133 us
  Pallas kernels  129 us (96%)
  local copies, waits for them, and re-layouts  4.24 us (3%)
    pallas_call x1, Pallas kernels, on_device(): pl.pallas_call(block_kernel, out_shape=[jax.ShapeDtypeStruct((tokens, WID...  129 us
    unnamed x2, local copies, waits for them, and re-layouts  4.24 us

profile of v2, /device:TPU:0, one launch (start us, length us, event | category | flops | bytes accessed | tf_op | source)
XLA Modules:
  0.0 133.3 jit_solution(5665335996587091224)
XLA Ops:
  0.0 2.0 %copy.14 = bf16[1,2048,80]{2,1,0:T(8,128)(2,1)} copy(bf16[1,2048,80]{1,2,0:T(8,128)(2,1)} %param.13) | data formatting | bytes 655360 | tf_op args[0]
  2.0 129.1 %shard_map.127 = bf16[512,1024]{1,0:T(8,128)(2,1)} custom-call(s32[1,4]{1,0:T(1,128)} %lengths_ref.1, bf16[2048,80]{1,0:T(8,128)(2,1)} %bitcast.6, f32[3,3,256]{2,1,0:T(4,128)} %w_first_ref.1, f32[1,1024]{1,0:T(1,128)} %bitcast.7, f32[1,1024]{1,0:T(1,128)} %bitcast.8, f32[9,1024]{1,0:T(8,128)} %w_depth_ref.1, f32[1,1024]{1,0:T(1,128)} %bitcast.9, ...), custom_call_target="tpu_custom_call" | custom-call | tf_op jit(solution)/shard_map/pallas_call | solution.py:447
  131.1 2.3 %copy.16 = bf16[1,512,1024]{2,1,0:T(8,128)(2,1)} copy(bf16[1,512,1024]{2,1,0:T(8,128)(2,1)} %bitcast.5) | data formatting | bytes 2097152

commit v3 on v2

--- a/solution.py
+++ b/solution.py
@@ -20,16 +20,26 @@
 
 ORDERS = (("x", "y", "z"), ("y", "z", "x"), ("z", "x", "y"))
 CHUNKS = (
-    (0, 0, 256, 0),
+    (0, 0, 128, 0), (0, 128, 128, 1),
     (1, 0, 256, 0), (1, 256, 384, 1), (1, 640, 384, 2),
     (2, 0, 1024, 0), (2, 1024, 1024, 1), (2, 2048, 1024, 2),
     (3, 0, 1024, 0), (4, 0, 384, 0), (5, 0, 1024, 1), (4, 384, 384, 1), (4, 768, 1280, 2),
 )
-PHASES = ((0,), (1, 2, 3), (4, 5, 6), (7, 8, 9, 10, 11))
-LOOP_STEPS = {
-    0: ((1, 3),), 1: ((2, 2),), 2: ((1, 4),), 3: ((3, 1),), 4: ((2, 3),), 6: ((2, 4), (3, 2)),
-    7: ((1, 5),), 9: ((3, 3),), 11: ((1, 6), (3, 4)), 12: ((2, 5),), 14: ((1, 7),), 16: ((2, 6),),
-    17: ((3, 5),), 19: ((2, 7),),
+PHASES = ((0, 1), (2, 3, 4), (5, 6, 7), (8, 9, 10, 11, 12))
+DIRECT = (
+    ((), (0, 1, 2)), ((0, 1, 2), (3, 4, 5)), ((3, 4, 5), (6, 7, 8, 9)), ((6, 7, 8), (10, 11, 12)),
+    ((9, 10, 11, 12), ()),
+)
+FORWARDED = (
+    ((), (0, 1, 2)), ((0, 1, 2), (3, 4)), ((3, 4), (5, 6)), ((5, 6), (7, 8, 11)),
+    ((7, 8), (9, 10, 12, 13)), ((9, 10), (14,)), ((11, 12, 13, 14), ()),
+)
+FIRST_STEPS = {
+    0: ((0, 2),), 1: ((2, 1),), 2: ((1, 2),), 5: ((3, 1),), 8: ((0, 3),), 9: ((2, 2),), 12: ((1, 3),),
+    14: ((3, 2),), 16: ((2, 3),), 18: ((0, 4),), 19: ((1, 4),),
+}
+SECOND_STEPS = {
+    1: ((3, 3),), 3: ((2, 4),), 8: ((3, 4),), 11: ((1, 5),), 18: ((1, 6),), 19: ((2, 5),),
 }
 SLOTS = 15
 
@@ -105,11 +115,18 @@
         array, column, columns, order = CHUNKS[chunk]
         axes = ORDERS[order]
         target = None
+        direct = chunk in PHASES[0]
+        siblings = 9 if direct else 11
         if slot < 3:
             target = self.near[axes[0], (1, 3, 2)[slot]]
             source = self.shards[array].at[:, pl.ds(column, columns)]
             place = self.view(chunk, 1, self.here)
-        elif slot < 11:
+        elif slot < siblings and direct:
+            stage = 2 if slot < 6 else 3
+            target = self.near[axes[stage - 1], (1, 3, 2)[slot % 3]]
+            source = self.view(chunk, stage, self.here)
+            place = source
+        elif slot < siblings:
             stage = 2 if slot < 7 else 3
             axis = axes[stage - 1]
             at = (slot - 3) % 4
@@ -121,7 +138,7 @@
             place = source
         else:
             axis = axes[2]
-            at = slot - 11
+            at = slot - siblings
             source = self.view(chunk, 3, self.here if at == 0 else self.near[axis, (3, 1, 2)[at - 1]])
             place = source
         where = self.device(self.here, 1 - self.core) if target is None else self.device(target, self.core)
@@ -131,8 +148,7 @@
         )
 
     def step(self, phase, number):
-        awaited = ((), (0, 1, 2), (3, 4), (5, 6), (7, 8), (9, 10), (11, 12, 13, 14))[number - 1]
-        started = ((0, 1, 2), (3, 4), (5, 6), (7, 8, 11), (9, 10, 12, 13), (14,), ())[number - 1]
+        awaited, started = (DIRECT if phase == 0 else FORWARDED)[number - 1]
         for chunk in PHASES[phase]:
             for slot in awaited:
                 self.copy(chunk, slot).wait_recv()
@@ -141,17 +157,17 @@
 
     def finish(self):
         for chunk in range(len(CHUNKS)):
-            for slot in range(SLOTS):
+            for slot in range(13 if chunk in PHASES[0] else SLOTS):
                 self.copy(chunk, slot).wait_send()
 
 
 def block_kernel(
     lengths_ref, mel_ref, w_first_ref, gain_attn_ref, gain_conv_ref, w_depth_ref, gain_out_ref,
     ws_shard, wp_shard, wq_shard, wo_shard, wi_shard, wu_shard,
-    out_ref,
-    edge, melf, x_ref, band, ws, wp, wq, wo, wi, wu, w2, w2s, even, odd, sub,
+    out_ref, spilled,
+    edge, melf, x_ref, band, ws, wp, wq, wo, wi, wu, w2, w2s, pairs, sub,
     hidden, normed, query, keyval, bias, context, extended,
-    send_sems, recv_sems, own_sems, halo_send, halo_recv,
+    send_sems, recv_sems, own_sems, halo_send, halo_recv, spill_sems, fetch_sems,
 ):
     tokens = mel_ref.shape[0] // 4
     channels = w_first_ref.shape[-1]
@@ -178,7 +194,6 @@
 
     for array in range(6):
         own_copy(array).start()
-    pl.semaphore_wait(barrier, len(greeted))
 
     def pass_on(source, place, device, number):
         return pltpu.make_async_remote_copy(
@@ -191,21 +206,15 @@
         value = whole[:, :, :, :, :, pl.ds(start, 256)]
         return value.reshape(128 * whole.shape[4], 256)
 
-    gather.step(0, 1)
-    edge_copy = pass_on(mel_ref.at[pl.ds(4 * tokens - 8, 8), :], edge, after, 0)
-    edge_copy.start()
-    gather.step(1, 1)
-    gather.step(2, 1)
-    for array in range(6):
-        own_copy(array).wait()
-
     first = lengths_ref[0, 0]
     second = first + lengths_ref[0, 1]
     bounds = (first, second, second + lengths_ref[0, 2])
+    melf[8:, :] = mel_ref[...].astype(F32)
 
     row_at = lax.broadcasted_iota(jnp.int32, (256, channels), 0)
     low_part, r = row_at // 128, row_at % 128
-    at = r // SPAN
+    at = (r >= SPAN).astype(jnp.int32) + (r >= 2 * SPAN).astype(jnp.int32)
+    at = jnp.where(r >= 3 * SPAN, 3, at)
     column = r - SPAN * at
     spread = []
     for b in range(3):
@@ -216,7 +225,13 @@
             value = jnp.where(at == a, jnp.where(low_part == 0, top, w - top), value)
         spread.append(value)
 
-    gather.step(0, 2)
+    pl.semaphore_wait(barrier, len(greeted))
+    edge_copy = pass_on(mel_ref.at[pl.ds(4 * tokens - 8, 8), :], edge, after, 0)
+    edge_copy.start()
+    gather.step(0, 1)
+    gather.step(1, 1)
+    for array in range(6):
+        own_copy(array).wait()
 
     def make_band(f, carry):
         value = jnp.zeros((256, channels), F32)
@@ -225,14 +240,7 @@
         band[f] = value.astype(BF16)
         return carry
 
-    lax.fori_loop(0, QUARTER // 2, make_band, 0)
-    gather.step(0, 3)
-    lax.fori_loop(QUARTER // 2, QUARTER, make_band, 0)
-    gather.step(0, 4)
-    edge_copy.wait_recv()
-
-    melf[0:8, :] = edge[...].astype(F32)
-    melf[8:, :] = mel_ref[...].astype(F32)
+    lax.fori_loop(0, QUARTER, make_band, 0)
     frame_at = 4 * tokens * tm + 4 * lax.broadcasted_iota(jnp.int32, (tokens, bins), 0)
     seg_here = segments(frame_at, bounds, frames_all)
 
@@ -242,33 +250,68 @@
     def same(d):
         return (segments(frame_at + d, bounds, frames_all) == seg_here).astype(F32)
 
-    low2, up2 = same(-2), same(2)
-    rows = (
-        (frame(-3) * same(-3), frame(-2) * low2, frame(-1) * low2),
-        (frame(-1) * same(-1), frame(0), frame(1) * same(1)),
-        (frame(1) * up2, frame(2) * up2, frame(3) * same(3)),
-    )
     bin_at = lax.broadcasted_iota(jnp.int32, (bins, 256), 0)
     place = lax.broadcasted_iota(jnp.int32, (bins, 256), 1)
     half, within = place // 128, place % 128
-    for v in range(3):
+
+    def lay_out(v, frames):
         total = jnp.zeros((tokens, 256), F32)
         for a in range(3):
             taken = within - SPAN * a
             chosen = (taken >= 0) & (taken < SPAN) & (bin_at == 40 * half - 1 + taken)
-            total = total + dot(rows[v][a].astype(BF16), chosen.astype(F32).astype(BF16))
+            total = total + dot(frames[a].astype(BF16), chosen.astype(F32).astype(BF16))
         total = total.astype(BF16)
         for h in range(2):
             piece = total[:, 128 * h : 128 * (h + 1)]
             x_ref[h, v * tokens : (v + 1) * tokens, 0:128] = piece
             x_ref[h, v * tokens : (v + 1) * tokens, 128:256] = piece
-        if v == 0:
-            gather.step(0, 5)
-        if v == 1:
-            gather.step(0, 6)
-
-    gather.step(1, 2)
-    gather.step(0, 7)
+
+    up2 = same(2)
+    lay_out(2, (frame(1) * up2, frame(2) * up2, frame(3) * same(3)))
+    edge_copy.wait_recv()
+    melf[0:8, :] = edge[...].astype(F32)
+    low2 = same(-2)
+    lay_out(1, (frame(-1) * same(-1), frame(0), frame(1) * same(1)))
+    lay_out(0, (frame(-3) * same(-3), frame(-2) * low2, frame(-1) * low2))
+
+    def spill(pair, slot):
+        return pltpu.make_async_copy(pairs.at[slot], spilled.at[pair], spill_sems.at[slot])
+
+    def fetch(pair, slot):
+        return pltpu.make_async_copy(spilled.at[pair], pairs.at[slot], fetch_sems.at[slot])
+
+    def advance(at, steps):
+        for number, todo in steps.items():
+
+            @pl.when(at == number)
+            def _():
+                for phase, step in todo:
+                    gather.step(phase, step)
+
+    def first_step(pair, carry):
+        advance(pair, FIRST_STEPS)
+        h = pair // 10
+        f = 2 * pair - 20 * h
+        slot = pair % 3
+
+        @pl.when(pair >= 3)
+        def _():
+            spill(pair - 3, slot).wait()
+
+        for part in range(2):
+            for v in range(3):
+                made = dot(x_ref[h, v * tokens : (v + 1) * tokens, :], band[f + part])
+                pairs[slot, part, :, v * channels : (v + 1) * channels] = jnp.maximum(made, 0.0).astype(BF16)
+        spill(pair, slot).start()
+        return carry
+
+    lax.fori_loop(0, QUARTER, first_step, 0)
+    for pair in range(QUARTER - 3, QUARTER):
+        spill(pair, pair % 3).wait()
+    fetch(0, 0).start()
+    pairs[2, 1] = jnp.zeros(pairs.shape[2:], BF16)
+
+    gather.step(0, 5)
     depth = ws.shape[4]
 
     def unpack(i, carry):
@@ -283,38 +326,33 @@
             start = (3 * a + b) * channels
             w2s[b, a * channels : (a + 1) * channels, :] = w2[start : start + channels, :]
 
-    odd[1] = jnp.zeros(odd.shape[1:], BF16)
-
-    def conv_step(f2, carry):
-        for number, pairs in LOOP_STEPS.items():
-
-            @pl.when(f2 == number)
-            def _():
-                for phase, step in pairs:
-                    gather.step(phase, step)
-
-        h = f2 // 10
-        f = 2 * f2 - 20 * h
-        slot = f2 % 2
-        for part, target in ((0, even), (1, odd.at[slot])):
-            for v in range(3):
-                made = dot(x_ref[h, v * tokens : (v + 1) * tokens, :], band[f + part])
-                target[:, v * channels : (v + 1) * channels] = jnp.maximum(made, 0.0).astype(BF16)
-        total = dot(odd[1 - slot], w2s[0]) + dot(even[...], w2s[1]) + dot(odd[slot], w2s[2])
-        columns = pl.ds(pl.multiple_of(f2 * channels, channels), channels)
+    def second_step(pair, carry):
+        advance(pair, SECOND_STEPS)
+        slot = pair % 3
+        fetch(pair, slot).wait()
+
+        @pl.when(pair < QUARTER - 1)
+        def _():
+            fetch(pair + 1, (pair + 1) % 3).start()
+
+        total = dot(pairs[(pair + 2) % 3, 1], w2s[0]) + dot(pairs[slot, 0], w2s[1]) + dot(pairs[slot, 1], w2s[2])
+        columns = pl.ds(pl.multiple_of(pair * channels, channels), channels)
         sub[:, columns] = jnp.maximum(total, 0.0).astype(BF16)
         return carry
 
-    lax.fori_loop(0, QUARTER, conv_step, 0)
+    lax.fori_loop(0, QUARTER, second_step, 0)
+    gather.step(1, 7)
 
     def project(start):
         columns = pl.ds(start, 256)
         hidden[:, columns] = dot(sub[...], weight(1, start))
 
     over_columns(2, project)
-    gather.step(3, 6)
+    gather.step(3, 5)
+    gather.step(2, 6)
     over_columns(4, project, 2)
     norm_rows(hidden, gain_attn_ref, normed)
+    gather.step(2, 7)
 
     def mix_keyval(start):
         keyval[WINDOW : WINDOW + tokens, pl.ds(start, 256)] = dot(
@@ -330,7 +368,7 @@
     )
     for copy in halos:
         copy.start()
-    gather.step(3, 7)
+    gather.step(3, 6)
 
     def mix_query(start):
         query[:, pl.ds(start, 256)] = dot(normed[...], weight(2, start)).astype(BF16)
@@ -371,6 +409,8 @@
 
     lax.fori_loop(0, blocks, attend, 0)
 
+    gather.step(3, 7)
+
     def attend_out(start):
         columns = pl.ds(start, 256)
         hidden[:, columns] = hidden[:, columns] + dot(context[...], weight(3, start))
@@ -444,11 +484,14 @@
     shards = (w_second, w_proj, w_qkv, w_out, w_point_in, w_point_out)
     vmem = pl.BlockSpec(memory_space=pltpu.VMEM)
     hbm = pl.BlockSpec(memory_space=pl.ANY)
-    (encoded,) = pl.pallas_call(
+    encoded, _ = pl.pallas_call(
         block_kernel,
-        out_shape=[jax.ShapeDtypeStruct((tokens, WIDTH), BF16)],
+        out_shape=[
+            jax.ShapeDtypeStruct((tokens, WIDTH), BF16),
+            jax.ShapeDtypeStruct((QUARTER, 2, tokens, 3 * channels), BF16),
+        ],
         in_specs=[pl.BlockSpec(memory_space=pltpu.SMEM)] + [vmem] * 6 + [hbm] * 6,
-        out_specs=[vmem],
+        out_specs=[vmem, hbm],
         scratch_shapes=[
             pltpu.VMEM((8, bins), BF16),
             pltpu.VMEM((4 * tokens + 8, bins), F32),
@@ -457,8 +500,7 @@
             *[pltpu.VMEM((4, 4, 4, 2) + s.shape, BF16) for s in shards],
             pltpu.VMEM((9 * channels, channels), BF16),
             pltpu.VMEM((3, 3 * channels, channels), BF16),
-            pltpu.VMEM((tokens, 3 * channels), BF16),
-            pltpu.VMEM((2, tokens, 3 * channels), BF16),
+            pltpu.VMEM((3, 2, tokens, 3 * channels), BF16),
             pltpu.VMEM((tokens, QUARTER * channels), BF16),
             pltpu.VMEM((tokens, WIDTH), F32),
             pltpu.VMEM((tokens, WIDTH), BF16),
@@ -472,6 +514,8 @@
             pltpu.SemaphoreType.DMA((6,)),
             pltpu.SemaphoreType.DMA((5,)),
             pltpu.SemaphoreType.DMA((5,)),
+            pltpu.SemaphoreType.DMA((3,)),
+            pltpu.SemaphoreType.DMA((3,)),
         ],
         compiler_params=pltpu.CompilerParams(
             collective_id=0, has_side_effects=True, vmem_limit_bytes=VMEM_LIMIT

time: 134 us -> 113 us (0.84)
  Pallas kernels: 129 us -> 108 us
    pallas_call x1, Pallas kernels: 129 us -> 108 us  [on_device(): pl.pallas_call(block_kernel, out_shape=[jax.ShapeDtypeStruct((tokens, WID...]
where the time goes in v3:
time: 113 us
  Pallas kernels  108 us (96%)
  local copies, waits for them, and re-layouts  4.24 us (4%)
    pallas_call x1, Pallas kernels, on_device(): pl.pallas_call(block_kernel, out_shape=[jax.ShapeDtypeStruct((tokens, WID...  108 us
    unnamed x2, local copies, waits for them, and re-layouts  4.24 us

profile of v3, /device:TPU:0, one launch (start us, length us, event | category | flops | bytes accessed | tf_op | source)
XLA Modules:
  0.0 112.7 jit_solution(6041473269013247206)
XLA Ops:
  0.0 2.0 %copy.14 = bf16[1,2048,80]{2,1,0:T(8,128)(2,1)} copy(bf16[1,2048,80]{1,2,0:T(8,128)(2,1)} %param.13) | data formatting | bytes 655360 | tf_op args[0]
  2.0 108.5 %shard_map.127 = (bf16[512,1024]{1,0:T(8,128)(2,1)}, bf16[20,2,512,768]{3,2,1,0:T(8,128)(2,1)}) custom-call(s32[1,4]{1,0:T(1,128)} %lengths_ref.1, bf16[2048,80]{1,0:T(8,128)(2,1)} %bitcast.5, f32[3,3,256]{2,1,0:T(4,128)} %w_first_ref.1, f32[1,1024]{1,0:T(1,128)} %bitcast.7, f32[1,1024]{1,0:T(1,128)} %bitcast.8, f32[9,1024]{1,0:T(8,128)} %w_depth_ref.1, ...), custom_call_target="tpu_custom_call" | custom-call | tf_op jit(solution)/shard_map/pallas_call | solution.py:487
  110.5 2.3 %copy.16 = bf16[1,512,1024]{2,1,0:T(8,128)(2,1)} copy(bf16[1,512,1024]{2,1,0:T(8,128)(2,1)} %bitcast.6) | data formatting | bytes 2097152

commit v4 on v3

--- a/solution.py
+++ b/solution.py
@@ -11,37 +11,39 @@
 WINDOW = 128
 HEAD_DIM = 128
 QUARTER = 20
+KEPT = 6
+LEAD = 16
 SPAN = 41
 NORM_EPSILON = 1e-05
-VMEM_LIMIT = 62 * 2**20
+VMEM_LIMIT = 63 * 2**20
 BF16 = jnp.bfloat16
 F32 = jnp.float32
 MESH = pl.DeviceIdType.MESH
 
 ORDERS = (("x", "y", "z"), ("y", "z", "x"), ("z", "x", "y"))
+PLACES = ((0, 0), (1, 0), (2, 0), (3, 0), (3, WIDTH), (3, 3 * WIDTH))
 CHUNKS = (
     (0, 0, 128, 0), (0, 128, 128, 1),
     (1, 0, 256, 0), (1, 256, 384, 1), (1, 640, 384, 2),
     (2, 0, 1024, 0), (2, 1024, 1024, 1), (2, 2048, 1024, 2),
-    (3, 0, 1024, 0), (4, 0, 384, 0), (5, 0, 1024, 1), (4, 384, 384, 1), (4, 768, 1280, 2),
+    (3, 0, 1408, 0), (3, 1408, 1280, 1), (3, 2688, 1408, 2),
 )
-PHASES = ((0, 1), (2, 3, 4), (5, 6, 7), (8, 9, 10, 11, 12))
+PHASES = ((0, 1), (2, 3, 4), (5, 6, 7), (8, 9, 10))
 DIRECT = (
     ((), (0, 1, 2)), ((0, 1, 2), (3, 4, 5)), ((3, 4, 5), (6, 7, 8, 9)), ((6, 7, 8), (10, 11, 12)),
     ((9, 10, 11, 12), ()),
 )
 FORWARDED = (
-    ((), (0, 1, 2)), ((0, 1, 2), (3, 4)), ((3, 4), (5, 6)), ((5, 6), (7, 8, 11)),
-    ((7, 8), (9, 10, 12, 13)), ((9, 10), (14,)), ((11, 12, 13, 14), ()),
+    ((), (0, 1, 2)), ((0, 1, 2), (3, 4, 5)), ((3, 4, 5), (6, 7, 10)), ((6, 7), (8, 9, 11, 12)),
+    ((8, 9), (13,)), ((10, 11, 12, 13), ()),
 )
-FIRST_STEPS = {
-    0: ((0, 2),), 1: ((2, 1),), 2: ((1, 2),), 5: ((3, 1),), 8: ((0, 3),), 9: ((2, 2),), 12: ((1, 3),),
-    14: ((3, 2),), 16: ((2, 3),), 18: ((0, 4),), 19: ((1, 4),),
-}
-SECOND_STEPS = {
-    1: ((3, 3),), 3: ((2, 4),), 8: ((3, 4),), 11: ((1, 5),), 18: ((1, 6),), 19: ((2, 5),),
-}
-SLOTS = 15
+FIRST_STEPS = {0: ((0, 2),), 2: ((1, 2),), 3: ((2, 1),), 9: ((0, 3),), 11: ((2, 2),), 12: ((3, 1),), 15: ((1, 3),), 18: ((0, 4),), 19: ((2, 3), (3, 2))}
+SECOND_STEPS = {9: ((1, 4),), 14: ((2, 4),), 15: ((3, 3),), 19: ((1, 5),)}
+PROJECT_STEPS = {2: ((2, 5),)}
+KEYVAL_STEPS = {0: ((3, 4),)}
+QUERY_STEPS = {3: ((3, 5),)}
+ATTEND_STEPS = {}
+SLOTS = 14
 
 
 def dot(a, b):
@@ -70,12 +72,13 @@
     lax.fori_loop(0, source.shape[0] // step, body, 0)
 
 
-def over_columns(count, body, first=0):
+def over_columns(count, body, before=lambda n: None):
     def step(n, carry):
+        before(n)
         body(pl.multiple_of(n * 256, 256))
         return carry
 
-    lax.fori_loop(first, count, step, 0)
+    lax.fori_loop(0, count, step, 0)
 
 
 class Gather:
@@ -116,25 +119,23 @@
         axes = ORDERS[order]
         target = None
         direct = chunk in PHASES[0]
-        siblings = 9 if direct else 11
+        siblings = 9 if direct else 10
         if slot < 3:
             target = self.near[axes[0], (1, 3, 2)[slot]]
-            source = self.shards[array].at[:, pl.ds(column, columns)]
             place = self.view(chunk, 1, self.here)
-        elif slot < siblings and direct:
+            source = place if array == 3 else self.shards[array].at[:, pl.ds(column, columns)]
+        elif slot < 6 or (direct and slot < 9):
             stage = 2 if slot < 6 else 3
             target = self.near[axes[stage - 1], (1, 3, 2)[slot % 3]]
             source = self.view(chunk, stage, self.here)
             place = source
         elif slot < siblings:
-            stage = 2 if slot < 7 else 3
-            axis = axes[stage - 1]
-            at = (slot - 3) % 4
-            target = self.near[axis, (1, 3, 1, 3)[at]]
+            at = slot - 6
+            target = self.near[axes[2], (1, 3, 1, 3)[at]]
             if at < 2:
-                source = self.view(chunk, stage, self.here)
+                source = self.view(chunk, 3, self.here)
             else:
-                source = self.view(chunk, stage, self.near[axis, (3, 1)[at - 2]], at - 2)
+                source = self.view(chunk, 3, self.near[axes[2], (3, 1)[at - 2]], at - 2)
             place = source
         else:
             axis = axes[2]
@@ -165,7 +166,7 @@
     lengths_ref, mel_ref, w_first_ref, gain_attn_ref, gain_conv_ref, w_depth_ref, gain_out_ref,
     ws_shard, wp_shard, wq_shard, wo_shard, wi_shard, wu_shard,
     out_ref, spilled,
-    edge, melf, x_ref, band, ws, wp, wq, wo, wi, wu, w2, w2s, pairs, sub,
+    edge, melf, x_ref, band, ws, wp, wq, wr, w2, frames_made, carried, sub,
     hidden, normed, query, keyval, bias, context, extended,
     send_sems, recv_sems, own_sems, halo_send, halo_recv, spill_sems, fetch_sems,
 ):
@@ -177,7 +178,7 @@
     rec = lax.axis_index("rec")
     frames_all = mel_ref.shape[0] * count
     shards = (ws_shard, wp_shard, wq_shard, wo_shard, wi_shard, wu_shard)
-    wholes = (ws, wp, wq, wo, wi, wu)
+    wholes = (ws, wp, wq, wr)
     gather = Gather(shards, wholes, send_sems, recv_sems)
     after = {"rec": rec, "tm": (tm + 1) % count}
     before = {"rec": rec, "tm": (tm + count - 1) % count}
@@ -189,7 +190,9 @@
 
     def own_copy(array):
         here = gather.here
-        place = wholes[array].at[here["z"], here["x"], here["y"], gather.core]
+        whole, column = PLACES[array]
+        width = pl.ds(column, shards[array].shape[1])
+        place = wholes[whole].at[here["z"], here["x"], here["y"], gather.core, slice(None), width]
         return pltpu.make_async_copy(shards[array], place, own_sems.at[array])
 
     for array in range(6):
@@ -202,14 +205,17 @@
         )
 
     def weight(array, start):
-        whole = wholes[array]
+        whole, column = PLACES[array]
+        whole = wholes[whole]
+        start = pl.multiple_of(start + column, 128)
         value = whole[:, :, :, :, :, pl.ds(start, 256)]
         return value.reshape(128 * whole.shape[4], 256)
 
     first = lengths_ref[0, 0]
     second = first + lengths_ref[0, 1]
     bounds = (first, second, second + lengths_ref[0, 2])
-    melf[8:, :] = mel_ref[...].astype(F32)
+    melf[0 : 4 * LEAD, :] = jnp.zeros((4 * LEAD, bins), F32)
+    melf[4 * LEAD :, :] = mel_ref[...].astype(F32)
 
     row_at = lax.broadcasted_iota(jnp.int32, (256, channels), 0)
     low_part, r = row_at // 128, row_at % 128
@@ -241,44 +247,54 @@
         return carry
 
     lax.fori_loop(0, QUARTER, make_band, 0)
-    frame_at = 4 * tokens * tm + 4 * lax.broadcasted_iota(jnp.int32, (tokens, bins), 0)
-    seg_here = segments(frame_at, bounds, frames_all)
-
-    def frame(d):
-        return melf[pl.ds(8 + d, tokens, stride=4), :]
-
-    def same(d):
-        return (segments(frame_at + d, bounds, frames_all) == seg_here).astype(F32)
+    token_at = tokens * tm + lax.broadcasted_iota(jnp.int32, (tokens, 128), 0)
+    seg_here = segments(4 * token_at, bounds, frames_all)
+    for k, d in ((0, -2), (1, 2)):
+        carried[k] = (segments(4 * token_at + d, bounds, frames_all) == seg_here).astype(F32)
+
+    def laid_out(first_token, count, centre):
+        at = 4 * (tokens * tm + first_token + lax.broadcasted_iota(jnp.int32, (count, bins), 0)) + centre
+        own = segments(at, bounds, frames_all)
+        total = jnp.zeros((count, 256), F32)
+        for a in range(3):
+            start = 4 * (LEAD + first_token) + centre + a - 1
+            taken = melf[pl.ds(start, count, stride=4), :]
+            if a != 1:
+                taken = taken * (segments(at + a - 1, bounds, frames_all) == own).astype(F32)
+            column = within - SPAN * a
+            chosen = (column >= 0) & (column < SPAN) & (bin_at == 40 * half - 1 + column)
+            total = total + dot(taken.astype(BF16), chosen.astype(F32).astype(BF16))
+        return total.astype(BF16)
+
+    def lay_out(row, first_token, count, centre):
+        total = laid_out(first_token, count, centre)
+        for h in range(2):
+            piece = total[:, 128 * h : 128 * (h + 1)]
+            x_ref[h, row : row + count, 0:128] = piece
+            x_ref[h, row : row + count, 128:256] = piece
 
     bin_at = lax.broadcasted_iota(jnp.int32, (bins, 256), 0)
     place = lax.broadcasted_iota(jnp.int32, (bins, 256), 1)
     half, within = place // 128, place % 128
 
-    def lay_out(v, frames):
-        total = jnp.zeros((tokens, 256), F32)
-        for a in range(3):
-            taken = within - SPAN * a
-            chosen = (taken >= 0) & (taken < SPAN) & (bin_at == 40 * half - 1 + taken)
-            total = total + dot(frames[a].astype(BF16), chosen.astype(F32).astype(BF16))
-        total = total.astype(BF16)
-        for h in range(2):
-            piece = total[:, 128 * h : 128 * (h + 1)]
-            x_ref[h, v * tokens : (v + 1) * tokens, 0:128] = piece
-            x_ref[h, v * tokens : (v + 1) * tokens, 128:256] = piece
-
-    up2 = same(2)
-    lay_out(2, (frame(1) * up2, frame(2) * up2, frame(3) * same(3)))
+    lay_out(LEAD, 0, tokens, 2)
     edge_copy.wait_recv()
-    melf[0:8, :] = edge[...].astype(F32)
-    low2 = same(-2)
-    lay_out(1, (frame(-1) * same(-1), frame(0), frame(1) * same(1)))
-    lay_out(0, (frame(-3) * same(-3), frame(-2) * low2, frame(-1) * low2))
+    melf[4 * LEAD - 8 : 4 * LEAD, :] = edge[...].astype(F32)
+    lay_out(LEAD + tokens, 0, tokens, 0)
+    lay_out(0, -LEAD, LEAD, 2)
 
     def spill(pair, slot):
-        return pltpu.make_async_copy(pairs.at[slot], spilled.at[pair], spill_sems.at[slot])
-
-    def fetch(pair, slot):
-        return pltpu.make_async_copy(spilled.at[pair], pairs.at[slot], fetch_sems.at[slot])
+        source = frames_made.at[pl.ds(2 * slot, 2)]
+        return pltpu.make_async_copy(source, spilled.at[pair - KEPT - 3], spill_sems.at[slot - KEPT])
+
+    def slot_of(pair):
+        turn = pair % (KEPT + 3)
+        return jnp.where(turn < KEPT, turn, KEPT + (QUARTER - 1 - turn) % 3)
+
+    def fetch(pair):
+        number = pair - KEPT - 3
+        place = frames_made.at[pl.ds(2 * slot_of(pair), 2)]
+        return pltpu.make_async_copy(spilled.at[number], place, fetch_sems.at[number])
 
     def advance(at, steps):
         for number, todo in steps.items():
@@ -288,28 +304,32 @@
                 for phase, step in todo:
                     gather.step(phase, step)
 
-    def first_step(pair, carry):
-        advance(pair, FIRST_STEPS)
+    def first_step(job, carry):
+        advance(job, FIRST_STEPS)
+        stays = (job < 2 * KEPT) & (job % 2 == 1)
+        turn = jnp.where(job < 2 * KEPT, job // 2, job - KEPT)
+        pair = jnp.where(stays, turn, QUARTER - 1 - turn)
+        slot = jnp.where(stays, turn, KEPT + turn % 3)
+
+        @pl.when(jnp.logical_not(stays) & (turn >= 3))
+        def _():
+            spill(pair + 3, slot).wait()
+
         h = pair // 10
         f = 2 * pair - 20 * h
-        slot = pair % 3
-
-        @pl.when(pair >= 3)
+        for part in range(2):
+            made = dot(x_ref[h], band[f + part])
+            frames_made[2 * slot + part] = jnp.maximum(made, 0.0).astype(BF16)
+
+        @pl.when(jnp.logical_not(stays) & (pair >= KEPT + 3))
         def _():
-            spill(pair - 3, slot).wait()
-
-        for part in range(2):
-            for v in range(3):
-                made = dot(x_ref[h, v * tokens : (v + 1) * tokens, :], band[f + part])
-                pairs[slot, part, :, v * channels : (v + 1) * channels] = jnp.maximum(made, 0.0).astype(BF16)
-        spill(pair, slot).start()
+            spill(pair, slot).start()
+
         return carry
 
     lax.fori_loop(0, QUARTER, first_step, 0)
-    for pair in range(QUARTER - 3, QUARTER):
-        spill(pair, pair % 3).wait()
-    fetch(0, 0).start()
-    pairs[2, 1] = jnp.zeros(pairs.shape[2:], BF16)
+    nothing = 2 * (KEPT + 3)
+    frames_made[nothing] = jnp.zeros(frames_made.shape[1:], BF16)
 
     gather.step(0, 5)
     depth = ws.shape[4]
@@ -321,45 +341,55 @@
         return carry
 
     lax.fori_loop(0, 16, unpack, 0)
-    for a in range(3):
-        for b in range(3):
-            start = (3 * a + b) * channels
-            w2s[b, a * channels : (a + 1) * channels, :] = w2[start : start + channels, :]
-
     def second_step(pair, carry):
         advance(pair, SECOND_STEPS)
-        slot = pair % 3
-        fetch(pair, slot).wait()
-
-        @pl.when(pair < QUARTER - 1)
+
+        @pl.when((pair >= 2) & (pair < QUARTER - KEPT - 1))
         def _():
-            fetch(pair + 1, (pair + 1) % 3).start()
-
-        total = dot(pairs[(pair + 2) % 3, 1], w2s[0]) + dot(pairs[slot, 0], w2s[1]) + dot(pairs[slot, 1], w2s[2])
-        columns = pl.ds(pl.multiple_of(pair * channels, channels), channels)
-        sub[:, columns] = jnp.maximum(total, 0.0).astype(BF16)
+            fetch(pair + KEPT + 1).start()
+
+        @pl.when(pair >= KEPT + 3)
+        def _():
+            fetch(pair).wait()
+
+        last = jnp.where(pair == 0, nothing, 2 * slot_of(pair - 1) + 1)
+        used = (last, 2 * slot_of(pair), 2 * slot_of(pair) + 1)
+
+        def taps(a, first_row, rows):
+            total = None
+            for b in range(3):
+                start = (3 * a + b) * channels
+                made = dot(frames_made[used[b], first_row : first_row + rows, :], w2[start : start + channels, :])
+                total = made if total is None else total + made
+            return total
+
+        below = taps(0, 0, LEAD + tokens)[LEAD - 1 : LEAD - 1 + tokens]
+        centre = taps(1, LEAD + tokens, tokens)
+        above = taps(2, LEAD, tokens)
+        for part in range(channels // 128):
+            lanes = slice(part * 128, (part + 1) * 128)
+            total = centre[:, lanes] + below[:, lanes] * carried[0] + above[:, lanes] * carried[1]
+            columns = pl.ds(pl.multiple_of(pair * channels + part * 128, 128), 128)
+            sub[:, columns] = jnp.maximum(total, 0.0).astype(BF16)
         return carry
 
     lax.fori_loop(0, QUARTER, second_step, 0)
-    gather.step(1, 7)
+    gather.step(1, 6)
 
     def project(start):
         columns = pl.ds(start, 256)
         hidden[:, columns] = dot(sub[...], weight(1, start))
 
-    over_columns(2, project)
-    gather.step(3, 5)
+    over_columns(WIDTH // 256, project, lambda n: advance(n, PROJECT_STEPS))
+    norm_rows(hidden, gain_attn_ref, normed)
     gather.step(2, 6)
-    over_columns(4, project, 2)
-    norm_rows(hidden, gain_attn_ref, normed)
-    gather.step(2, 7)
 
     def mix_keyval(start):
         keyval[WINDOW : WINDOW + tokens, pl.ds(start, 256)] = dot(
             normed[...], weight(2, WIDTH + start)
         ).astype(BF16)
 
-    over_columns(2 * WIDTH // 256, mix_keyval)
+    over_columns(2 * WIDTH // 256, mix_keyval, lambda n: advance(n, KEYVAL_STEPS))
     halos = (
         pass_on(keyval.at[pl.ds(tokens, WINDOW), :], keyval.at[pl.ds(0, WINDOW), :], after, 1),
         pass_on(
@@ -368,12 +398,11 @@
     )
     for copy in halos:
         copy.start()
-    gather.step(3, 6)
 
     def mix_query(start):
         query[:, pl.ds(start, 256)] = dot(normed[...], weight(2, start)).astype(BF16)
 
-    over_columns(WIDTH // 256, mix_query)
+    over_columns(WIDTH // 256, mix_query, lambda n: advance(n, QUERY_STEPS))
 
     base = tokens * tm
     reach = 3 * WINDOW
@@ -384,6 +413,7 @@
 
     def attend(i, carry):
         block = (i + 1) % blocks
+        advance(i, ATTEND_STEPS)
 
         @pl.when(i == blocks - 2)
         def _():
@@ -395,21 +425,27 @@
         q_seg = segments(4 * (base + start + q_at), bounds, frames_all)
         k_seg = segments(4 * (base + start + k_at), bounds, frames_all)
         bias[...] = jnp.where(near & (q_seg == k_seg), 0.0, -1e30)
-        for head in range(HEADS):
-            own = slice(head * HEAD_DIM, (head + 1) * HEAD_DIM)
-            values = slice(WIDTH + head * HEAD_DIM, WIDTH + (head + 1) * HEAD_DIM)
-            scores = lax.dot_general(
+        lanes = [slice(head * HEAD_DIM, (head + 1) * HEAD_DIM) for head in range(HEADS)]
+        masked = bias[...]
+        scores = [
+            lax.dot_general(
                 query[q_rows, own], keyval[k_rows, own], (((1,), (1,)), ((), ())),
                 preferred_element_type=F32,
-            ) * HEAD_DIM ** (-0.5) + bias[...]
-            exped = jnp.exp(scores - jnp.max(scores, axis=-1, keepdims=True))
-            share = 1.0 / jnp.sum(exped, axis=-1, keepdims=True)
-            context[q_rows, own] = dot((exped * share).astype(BF16), keyval[k_rows, values]).astype(BF16)
+            ) * HEAD_DIM ** (-0.5) + masked
+            for own in lanes
+        ]
+        tops = [jnp.max(score, axis=-1, keepdims=True) for score in scores]
+        exped = [jnp.exp(score - top) for score, top in zip(scores, tops)]
+        shares = [1.0 / jnp.sum(e, axis=-1, keepdims=True) for e in exped]
+        for head, own in enumerate(lanes):
+            values = slice(WIDTH + head * HEAD_DIM, WIDTH + (head + 1) * HEAD_DIM)
+            probabilities = (exped[head] * shares[head]).astype(BF16)
+            context[q_rows, own] = dot(probabilities, keyval[k_rows, values]).astype(BF16)
         return carry
 
     lax.fori_loop(0, blocks, attend, 0)
 
-    gather.step(3, 7)
+    gather.step(3, 6)
 
     def attend_out(start):
         columns = pl.ds(start, 256)
@@ -488,19 +524,20 @@
         block_kernel,
         out_shape=[
             jax.ShapeDtypeStruct((tokens, WIDTH), BF16),
-            jax.ShapeDtypeStruct((QUARTER, 2, tokens, 3 * channels), BF16),
+            jax.ShapeDtypeStruct((QUARTER - KEPT - 3, 2, LEAD + 2 * tokens, channels), BF16),
         ],
         in_specs=[pl.BlockSpec(memory_space=pltpu.SMEM)] + [vmem] * 6 + [hbm] * 6,
         out_specs=[vmem, hbm],
         scratch_shapes=[
             pltpu.VMEM((8, bins), BF16),
-            pltpu.VMEM((4 * tokens + 8, bins), F32),
-            pltpu.VMEM((2, 3 * tokens, 256), BF16),
+            pltpu.VMEM((4 * (LEAD + tokens), bins), F32),
+            pltpu.VMEM((2, LEAD + 2 * tokens, 256), BF16),
             pltpu.VMEM((QUARTER, 256, channels), BF16),
-            *[pltpu.VMEM((4, 4, 4, 2) + s.shape, BF16) for s in shards],
+            *[pltpu.VMEM((4, 4, 4, 2) + s.shape, BF16) for s in shards[:3]],
+            pltpu.VMEM((4, 4, 4, 2, w_out.shape[0], 4 * WIDTH), BF16),
             pltpu.VMEM((9 * channels, channels), BF16),
-            pltpu.VMEM((3, 3 * channels, channels), BF16),
-            pltpu.VMEM((3, 2, tokens, 3 * channels), BF16),
+            pltpu.VMEM((2 * (KEPT + 3) + 1, LEAD + 2 * tokens, channels), BF16),
+            pltpu.VMEM((2, tokens, 128), F32),
             pltpu.VMEM((tokens, QUARTER * channels), BF16),
             pltpu.VMEM((tokens, WIDTH), F32),
             pltpu.VMEM((tokens, WIDTH), BF16),
@@ -515,7 +552,7 @@
             pltpu.SemaphoreType.DMA((5,)),
             pltpu.SemaphoreType.DMA((5,)),
             pltpu.SemaphoreType.DMA((3,)),
-            pltpu.SemaphoreType.DMA((3,)),
+            pltpu.SemaphoreType.DMA((QUARTER - KEPT - 3,)),
         ],
         compiler_params=pltpu.CompilerParams(
             collective_id=0, has_side_effects=True, vmem_limit_bytes=VMEM_LIMIT

time: 113 us -> 104 us (0.920)
  Pallas kernels: 108 us -> 99.3 us
    pallas_call x1, Pallas kernels: 108 us -> 99.3 us  [on_device(): pl.pallas_call(block_kernel, out_shape=[jax.ShapeDtypeStruct((tokens, WID...]
where the time goes in v4:
time: 104 us
  Pallas kernels  99.3 us (95%)
  local copies, waits for them, and re-layouts  4.24 us (4%)
    pallas_call x1, Pallas kernels, on_device(): pl.pallas_call(block_kernel, out_shape=[jax.ShapeDtypeStruct((tokens, WID...  99.3 us
    unnamed x2, local copies, waits for them, and re-layouts  4.24 us

profile of v4, /device:TPU:0, one launch (start us, length us, event | category | flops | bytes accessed | tf_op | source)
XLA Modules:
  0.0 103.5 jit_solution(2597106979949175730)
XLA Ops:
  0.0 2.0 %copy.14 = bf16[1,2048,80]{2,1,0:T(8,128)(2,1)} copy(bf16[1,2048,80]{1,2,0:T(8,128)(2,1)} %param.13) | data formatting | bytes 655360 | tf_op args[0]
  2.0 99.3 %shard_map.127 = (bf16[512,1024]{1,0:T(8,128)(2,1)}, bf16[11,2,1040,256]{3,2,1,0:T(8,128)(2,1)}) custom-call(s32[1,4]{1,0:T(1,128)} %lengths_ref.1, bf16[2048,80]{1,0:T(8,128)(2,1)} %bitcast.5, f32[3,3,256]{2,1,0:T(4,128)} %w_first_ref.1, f32[1,1024]{1,0:T(1,128)} %bitcast.7, f32[1,1024]{1,0:T(1,128)} %bitcast.8, f32[9,1024]{1,0:T(8,128)} %w_depth_ref.1, ...), custom_call_target="tpu_custom_call" | custom-call | tf_op jit(solution)/shard_map/pallas_call | solution.py:523
  101.3 2.3 %copy.16 = bf16[1,512,1024]{2,1,0:T(8,128)(2,1)} copy(bf16[1,512,1024]{2,1,0:T(8,128)(2,1)} %bitcast.6) | data formatting | bytes 2097152
